TPU v7x, 32 devices: a whole 2x2x4 slice. The times are simulated.
32 devices in a mesh: parts: 2 (over x), freq: 16 (over z, y, core).
Axes of the slice: x: 2, y: 2, z: 4, core: 2. Of those that a mesh axis runs over, the one named last changes fastest.
Arguments:
- records: bfloat16 [2, 1024, 192, 128], P('parts', None, 'freq'), parts along dimension 0, may hold values from -6 to 6
- wavelet: float32 [2, 1024], P('parts'), parts along dimension 0, may hold values from -6 to 6
- offsets: int32 [2, 12, 8, 2], P('parts'), parts along dimension 0, may hold values from 0 to 15
- classes: int32 [8, 192, 128], P('parts'), parts along dimension 0, may hold values from 0 to 31
- coefficients: float32 [32, 64, 2, 9], P(None, 'freq'), may hold values from -2.5 to 2.5
Outputs:
- image: float32 [8, 192, 128], P('parts', 'freq'), parts along dimension 0
There are 2 independent parts, one for each index of `parts`. A program takes and returns all parts, laid end to end along the dimension named above; an argument that names none is the same for every part. Nothing has to cross between parts.
Inputs may be any that keep to these rules, and one draw needn't show every extreme that they name: Each shot has exactly one source in every 16 x 16 block of the surface, at these offsets inside the block.
All inputs are finite; a program needn't handle non-finite values.
Results may differ from a plain program's by a relative error of at most 0.0023.
Values sent between devices are 32-bit elements; how exact they have to be, the bound alone decides.
A program may use at most 128 MiB of HBM per device.

v0:
```python
import functools
import math

import jax
import jax.numpy as jnp
import numpy as np
from jax import lax
from jax.experimental import pallas as pl
from jax.experimental.pallas import tpu as pltpu
from jax.sharding import PartitionSpec as P

NF = 64
SPACING = 16
LANES = 128
SUBS = 8
NODES = (0.0, 1.0)


first_bin = 4


def dft_rows(count, record_duration):
    slots = np.arange(count, dtype=np.int64) + first_bin
    moments = np.arange(record_duration, dtype=np.int64)
    phase = (slots[:, None] * moments[None, :] % record_duration).astype(np.float32)
    phase = phase * np.float32(2.0 * math.pi / record_duration)
    scaling = np.float32(1.0 / math.sqrt(record_duration))
    return np.cos(phase) * scaling, -np.sin(phase) * scaling


def basis_change(degrees):
    poly = np.polynomial.Polynomial
    basis = [poly([1.0])]
    for j in range(degrees - 1):
        basis.append(basis[-1] * poly([-16.0 * NODES[j % 2], 16.0]))
    matrix = np.zeros((degrees, degrees))
    for j, b in enumerate(basis):
        matrix[: len(b.coef), j] = b.coef
    out = np.zeros((degrees, degrees))
    for k in range(degrees):
        shifted = np.polynomial.Chebyshev.basis(k).convert(kind=poly)(poly([-1.0, 2.0]))
        coef = np.zeros(degrees)
        coef[: len(shifted.coef)] = shifted.coef
        out[:, k] = np.linalg.solve(matrix, coef)
    return out


def iotas():
    lane = lax.broadcasted_iota(jnp.int32, (SUBS, LANES), 1)
    sub = lax.broadcasted_iota(jnp.int32, (SUBS, LANES), 0)
    return lane, sub


def pick(table, index):
    along_lanes = lax.GatherDimensionNumbers(
        offset_dims=(),
        collapsed_slice_dims=(1,),
        start_index_map=(1,),
        operand_batching_dims=(0,),
        start_indices_batching_dims=(0,),
    )
    return lax.gather(
        table,
        index[..., None],
        along_lanes,
        slice_sizes=(1, 1),
        mode=lax.GatherScatterMode.PROMISE_IN_BOUNDS,
    )


def row_of(tab, part, k):
    return jnp.broadcast_to(tab[part, pl.ds(k, 1), :], (SUBS, LANES))


def lane_classes(classes, idx, flat, group, class_count):
    depths, nx, ny = idx.shape[:3]
    blocks = LANES // group
    lane, _ = iotas()
    places = [(d, x) for d in range(depths) for x in range(nx)]
    for n in range(0, len(places), group):
        some = places[n : n + group]
        rows = [classes[d, pl.ds(x, blocks, stride=nx), :] for d, x in some]
        slot = n // group % 2
        flat[slot] = jnp.transpose(jnp.concatenate(rows, axis=0).astype(jnp.float32))
        for y in range(ny):
            line = flat[slot, pl.ds(y, SUBS, stride=ny), :].astype(jnp.int32)
            for i, (d, x) in enumerate(some):
                idx[d, x, y] = pick(line, lane // group + i * blocks) + lane % group * class_count


def degree_pass(cur, planes, acc, tab, k, idx, node, group, nx, ny):
    lane, sub = iotas()
    low, high = lane >= group, lane < LANES - group
    first, last = sub >= 1, sub < SUBS - 1
    gr, gi = row_of(tab, 0, k), row_of(tab, 1, k)

    def along_x(c, y):
        v = [cur[c, x, y] for x in range(nx)]
        before = jnp.where(low, pltpu.roll(v[nx - 1], group, 1), 0.0)
        after = jnp.where(high, pltpu.roll(v[0], LANES - group, 1), 0.0)
        ext = [before] + v + [after]
        pair = [ext[i] + ext[i + 1] for i in range(nx + 1)]
        return [pair[i] + pair[i + 1] for i in range(nx)]

    u, q, u_first = [], [], []
    for c in range(planes):
        end = along_x(c, ny - 1)
        prev = [jnp.where(first, pltpu.roll(e, 1, 0), 0.0) for e in end]
        start = along_x(c, 0)
        u.append(start)
        u_first.append(start)
        q.append([a + b for a, b in zip(prev, start)])
    for y in range(ny):
        made = []
        for c in range(planes):
            if y < ny - 1:
                nxt = along_x(c, y + 1)
            else:
                nxt = [jnp.where(last, pltpu.roll(e, SUBS - 1, 0), 0.0) for e in u_first[c]]
            q_next = [a + b for a, b in zip(u[c], nxt)]
            total = [a + b for a, b in zip(q[c], q_next)]
            if node:
                total = [t - (16.0 * node) * cur[c, x, y] for x, t in enumerate(total)]
            for x in range(nx):
                cur[c, x, y] = total[x]
            made.append(total)
            u[c], q[c] = nxt, q_next
        for x in range(nx):
            hr, hi = pick(gr, idx[x, y]), pick(gi, idx[x, y])
            if planes == 2:
                re, im = made[0][x], made[1][x]
                acc[0, x, y] = acc[0, x, y] + (hr * re - hi * im)
                acc[1, x, y] = acc[1, x, y] + (hr * im + hi * re)
            else:
                acc[0, x, y] = acc[0, x, y] + hr * made[0][x]
                acc[1, x, y] = acc[1, x, y] + hi * made[0][x]


def all_degrees(cur, planes, acc, tab, idx, group, nx, ny, degrees):
    def two(j, carry):
        degree_pass(cur, planes, acc, tab, 2 * j + 1, idx, NODES[0], group, nx, ny)
        degree_pass(cur, planes, acc, tab, 2 * j + 2, idx, NODES[1], group, nx, ny)
        return carry

    lax.fori_loop(0, (degrees - 1) // 2, two, 0)
    if degrees % 2 == 0:
        degree_pass(cur, planes, acc, tab, degrees - 1, idx, NODES[0], group, nx, ny)


def degree_zero(cur, acc, tab, idx, nx, ny, load):
    gr, gi = row_of(tab, 0, 0), row_of(tab, 1, 0)

    def row(y, carry):
        for x in range(nx):
            re, im = load(x, y)
            cur[0, x, y] = re
            cur[1, x, y] = im
            hr, hi = pick(gr, idx[x, y]), pick(gi, idx[x, y])
            acc[0, x, y] = hr * re - hi * im
            acc[1, x, y] = hr * im + hi * re
        return carry

    lax.fori_loop(0, ny, row, 0, unroll=2)


def source_kernel(group, class_count, off_ref, wave_ref, tab, classes, out, idx, cur, flat):
    depths, nx, ny = idx.shape[:3]
    degrees = tab.shape[1]
    lane, _ = iotas()
    lane_classes(classes, idx, flat, group, class_count)
    gr, gi = row_of(tab, 0, 0), row_of(tab, 1, 0)
    row_x = [lane // group * nx + x for x in range(nx)]
    off_x = [pick(off_ref[0], r // SPACING) for r in row_x]
    off_y = [pick(off_ref[1], r // SPACING) for r in row_x]

    def spike_row(y, carry):
        for x in range(nx):
            hit = (row_x[x] % SPACING == off_x[x]) & (off_y[x] == y)
            v = jnp.where(hit, 1.0, 0.0)
            cur[0, x, y] = v
            out[0, 0, x, y] = pick(gr, idx[0, x, y]) * v
            out[0, 1, x, y] = pick(gi, idx[0, x, y]) * v
        return carry

    lax.fori_loop(0, ny, spike_row, 0, unroll=2)
    all_degrees(cur, 1, out.at[0], tab, idx.at[0], group, nx, ny, degrees)
    wr, wi = jnp.zeros((SUBS, LANES), jnp.float32), jnp.zeros((SUBS, LANES), jnp.float32)
    for f in range(group):
        wr = jnp.where(lane % group == f, wave_ref[f], wr)
        wi = jnp.where(lane % group == f, -wave_ref[group + f], wi)

    def wave_row(y, carry):
        for x in range(nx):
            re, im = out[0, 0, x, y], out[0, 1, x, y]
            out[0, 0, x, y] = wr * re - wi * im
            out[0, 1, x, y] = wr * im + wi * re
        return carry

    lax.fori_loop(0, ny, wave_row, 0, unroll=2)

    def depth(d, carry):
        def load(x, y):
            return out[d - 1, 0, x, y], out[d - 1, 1, x, y]

        degree_zero(cur, out.at[d], tab, idx.at[d], nx, ny, load)
        all_degrees(cur, 2, out.at[d], tab, idx.at[d], group, nx, ny, degrees)
        return carry

    lax.fori_loop(1, depths, depth, 0)


def receiver_kernel(group, begin, steps, received, src, tab, idx, out, acc, cur, flat, turned):
    nx, ny = idx.shape[1:3]
    degrees = tab.shape[1]
    if begin == 0:
        senders = received.shape[0]
        sub3 = lax.broadcasted_iota(jnp.int32, (senders, SUBS, LANES), 1)
        upper = sub3 < group
        for x in range(nx):
            a, b = received[:, x], received[:, nx + x]
            parts = (
                jnp.where(upper, a, pltpu.roll(b, group, 1)),
                jnp.where(upper, pltpu.roll(a, group, 1), b),
            )
            for r in range(2):
                flat[r] = jnp.transpose(parts[r].reshape(LANES, LANES))
                for y in range(ny):
                    acc[r, x, y] = flat[r, pl.ds(y, SUBS, stride=ny), :]
    halves = 2
    owners = LANES // (group * halves)
    stride = out.shape[0] // owners

    def depth(n, carry):
        d = begin + n
        field = received if begin else acc
        degree_zero(
            cur, acc, tab, idx.at[d], nx, ny, lambda x, y: (field[0, x, y], field[1, x, y])
        )
        all_degrees(cur, 2, acc, tab, idx.at[d], group, nx, ny, degrees)
        for x in range(nx):
            for y in range(ny):
                v = src[d, 0, x, y] * acc[0, x, y] - src[d, 1, x, y] * acc[1, x, y]
                shift = 1
                while shift < group:
                    v = v + pltpu.roll(v, shift, 1)
                    shift *= 2
                flat[x % 2, pl.ds(y, SUBS, stride=ny), :] = v
            turned[x % 2] = jnp.transpose(flat[x % 2])
            for b in range(halves):
                at = (n * halves + b) * nx + x
                for c in range(2):
                    lane = (c * halves + b) * group + group - 1
                    out[pl.ds(c * (owners // 2) * stride + at, owners // 2, stride=stride), :] = (
                        turned[x % 2, pl.ds(lane, owners // 2, stride=2 * halves * group), :]
                    )
        return carry

    if steps == 1:
        depth(0, 0)
    else:
        lax.fori_loop(0, steps, depth, 0)


def exchange_kernel(ranks, image, out, half, summed, slots, pair_sems, send_sem, recv_sem):
    me = lax.axis_index("freq")
    core, chip = lax.rem(me, 2), me // 2
    other = chip * 2 + 1 - core
    chips = ranks // 2
    tile, depths = out.shape[:2]

    def reach(k):
        return lax.rem(chip + k, chips) * 2 + core

    barrier = pltpu.get_barrier_semaphore()
    for peer in [other] + [reach(k) for k in range(1, chips)]:
        pl.semaphore_signal(
            barrier, inc=1, device_id={"freq": peer}, device_id_type=pl.DeviceIdType.MESH
        )
    pl.semaphore_wait(barrier, chips)
    swap = pltpu.make_async_remote_copy(
        src_ref=image.at[1 - core],
        dst_ref=half,
        send_sem=pair_sems.at[0],
        recv_sem=pair_sems.at[1],
        device_id={"freq": other},
        device_id_type=pl.DeviceIdType.MESH,
    )
    swap.start()
    swap.wait()
    copies = []
    for j in range(chips):
        summed[j] = image[core, j] + half[j]
    for k in range(1, chips):
        copy = pltpu.make_async_remote_copy(
            src_ref=summed.at[lax.rem(chip + k, chips)],
            dst_ref=slots.at[k - 1],
            send_sem=send_sem.at[k - 1],
            recv_sem=recv_sem.at[k - 1],
            device_id={"freq": reach(k)},
            device_id_type=pl.DeviceIdType.MESH,
        )
        copy.start()
        copies.append(copy)
    total = summed[chip]
    for k in range(1, chips):
        copies[k - 1].wait_recv()
        total = total + slots[k - 1]
    for d in range(depths):
        out[:, d, :] = total[d * tile : (d + 1) * tile]
    for copy in copies:
        copy.wait_send()


def fast_device(records, wavelet, offsets, classes, coefficients):
    _, record_duration, tile_rows, width = records.shape
    depths, height, _ = classes.shape
    class_count, group, _, degrees = coefficients.shape
    ranks = height // tile_rows
    nx, ny = group * height // LANES, width // SUBS
    cos_rows, sin_rows = dft_rows(NF, record_duration)
    pair = np.stack(
        [cos_rows.reshape(ranks, group, -1), -sin_rows.reshape(ranks, group, -1)], axis=1
    ).reshape(ranks, 2 * group, record_duration)
    narrow = jnp.asarray(pair).astype(jnp.bfloat16)
    spectra = jnp.einsum(
        "jqt,txy->jxqy", narrow, records[0], preferred_element_type=jnp.float32
    )
    received = lax.all_to_all(spectra, "freq", split_axis=0, concat_axis=0, tiled=True)

    mine = lax.dynamic_index_in_dim(jnp.asarray(pair), lax.axis_index("freq"), 0, keepdims=False)
    wave = jnp.sum(mine * wavelet, axis=1)
    off = offsets[0].transpose(2, 1, 0)
    off = jnp.pad(off, ((0, 0), (0, 0), (0, LANES - off.shape[2])))
    change = jnp.asarray(basis_change(degrees), jnp.float32)
    tab = jnp.einsum("jk,cfrk->rjfc", change, coefficients, precision=lax.Precision.HIGHEST)
    tab = tab.reshape(2, degrees, group * class_count)
    tab = jnp.pad(tab, ((0, 0), (0, 0), (0, LANES - group * class_count)))

    plane = (2, nx, ny, SUBS, LANES)
    square = pltpu.VMEM((2, LANES, LANES), jnp.float32)
    vmem = pl.BlockSpec(memory_space=pltpu.VMEM)
    smem = pl.BlockSpec(memory_space=pltpu.SMEM)
    source, index = pl.pallas_call(
        functools.partial(source_kernel, group, class_count),
        out_shape=[
            jax.ShapeDtypeStruct((depths,) + plane, jnp.float32),
            jax.ShapeDtypeStruct((depths,) + plane[1:], jnp.int32),
        ],
        in_specs=[vmem, smem, vmem, vmem],
        out_specs=[vmem] * 2,
        scratch_shapes=[pltpu.VMEM(plane, jnp.float32), square],
        cost_estimate=pl.CostEstimate(flops=10**9, bytes_accessed=6 * 10**7, transcendentals=0),
        name="source_steps",
    )(off, wave, tab, classes)

    def receive(begin, end, field):
        rows = -(-(end - begin) * tile_rows // SUBS) * SUBS
        return pl.pallas_call(
            functools.partial(receiver_kernel, group, begin, end - begin),
            out_shape=jax.ShapeDtypeStruct((ranks * rows, width), jnp.float32),
            in_specs=[vmem] * 4,
            out_specs=vmem,
            scratch_shapes=[pltpu.VMEM(plane, jnp.float32)] * 2 + [square, square],
            cost_estimate=pl.CostEstimate(flops=10**9, bytes_accessed=6 * 10**7, transcendentals=0),
            name="receiver_steps",
        )(field, source, tab, index)

    image = receive(0, depths, received)
    rows = image.shape[0] // ranks
    tiles = pl.pallas_call(
        functools.partial(exchange_kernel, ranks),
        out_shape=jax.ShapeDtypeStruct((tile_rows, depths, width), jnp.float32),
        in_specs=[vmem],
        out_specs=vmem,
        scratch_shapes=[
            pltpu.VMEM((ranks // 2, rows, width), jnp.float32),
            pltpu.VMEM((ranks // 2, rows, width), jnp.float32),
            pltpu.VMEM((ranks // 2 - 1, rows, width), jnp.float32),
            pltpu.SemaphoreType.DMA((2,)),
            pltpu.SemaphoreType.DMA((ranks // 2 - 1,)),
            pltpu.SemaphoreType.DMA((ranks // 2 - 1,)),
        ],
        compiler_params=pltpu.CompilerParams(collective_id=0, has_side_effects=True),
        name="exchange_tiles",
    )(image.reshape(2, ranks // 2, rows, width))
    return tiles.transpose(1, 0, 2)


def dft_table(count, record_duration):
    spectral_slots = jnp.arange(count, dtype=jnp.int32) + first_bin
    clock_moments = jnp.arange(record_duration, dtype=jnp.int32)
    elementwise_multiple = spectral_slots[:, None] * clock_moments[None, :] % record_duration
    phase = elementwise_multiple.astype(jnp.float32) * (2.0 * math.pi / record_duration)
    scaling = 1.0 / math.sqrt(record_duration)
    stacked = jnp.stack([jnp.cos(phase), -jnp.sin(phase)], axis=1) * scaling
    return stacked.reshape(2 * count, record_duration)


def mcclellan(field):
    widths = [(0, 0)] * (field.ndim - 2) + [(1, 1), (1, 1)]
    zero_extended = jnp.pad(field, widths)
    along_x = (
        0.25 * zero_extended[..., :-2, :]
        + 0.5 * zero_extended[..., 1:-1, :]
        + 0.25 * zero_extended[..., 2:, :]
    )
    smoothed = 0.25 * along_x[..., :-2] + 0.5 * along_x[..., 1:-1] + 0.25 * along_x[..., 2:]
    return 2.0 * smoothed - field


def add_term(summed_terms, chebyshev, filters, degree):
    wavefield_polarity = jnp.array([1.0, -1.0], jnp.float32)[None, :, None, None, None]
    real_component = filters[:, 0, degree][:, None, None]
    im_part = filters[:, 1, degree][:, None, None] * wavefield_polarity
    cheb_re = chebyshev[:, :, :, 0]
    cheb_im = chebyshev[:, :, :, 1]
    return summed_terms + jnp.stack(
        [
            real_component * cheb_re - im_part * cheb_im,
            real_component * cheb_im + im_part * cheb_re,
        ],
        axis=3,
    )


def extrapolate(fields, filters):
    degrees = filters.shape[2]
    previous = fields
    current = mcclellan(fields)
    summed_terms = add_term(jnp.zeros_like(fields), previous, filters, 0)
    summed_terms = add_term(summed_terms, current, filters, 1)
    for degree in range(2, degrees):
        previous, current = (current, 2.0 * mcclellan(current) - previous)
        summed_terms = add_term(summed_terms, current, filters, degree)
    return summed_terms


def emitter_impulses(offsets, spacing, height, breadth):
    off_x = jnp.repeat(jnp.repeat(offsets[..., 0], spacing, axis=1), spacing, axis=2)
    off_y = jnp.repeat(jnp.repeat(offsets[..., 1], spacing, axis=1), spacing, axis=2)
    row_phase = jnp.arange(height, dtype=jnp.int32) % spacing
    col_phase = jnp.arange(breadth, dtype=jnp.int32) % spacing
    hits = (row_phase[None, :, None] == off_x) & (col_phase[None, None, :] == off_y)
    return hits.astype(jnp.float32)


def plain_device(records, wavelet, offsets, classes, coefficients):
    shot_count, record_duration, tile_rows, width_y = records.shape
    freq_local = coefficients.shape[1]
    fourier_matrix = dft_table(NF, record_duration)
    narrow_table = fourier_matrix.astype(jnp.bfloat16)
    spectra = jnp.stack(
        [
            jnp.dot(
                narrow_table,
                records[0].reshape(record_duration, tile_rows * width_y),
                preferred_element_type=jnp.float32,
            ).reshape(NF, 2, tile_rows, width_y)
        ],
        axis=1,
    )
    receivers = lax.all_to_all(spectra, "freq", split_axis=0, concat_axis=3, tiled=True)
    height = receivers.shape[3]
    wave_spec = (
        jnp.dot(wavelet, fourier_matrix.T, precision=lax.Precision.HIGHEST)
        .reshape(shot_count, NF, 2)
        .transpose(1, 0, 2)
    )
    first_freq = lax.axis_index("freq") * freq_local
    wave_local = lax.dynamic_slice_in_dim(wave_spec, first_freq, freq_local, 0)
    spikes = emitter_impulses(offsets, SPACING, height, width_y)
    source = wave_local[:, :, :, None, None] * spikes[None, :, None]
    fields = jnp.stack([source, receivers], axis=1)
    class_ids = jnp.arange(coefficients.shape[0], dtype=jnp.int32)
    migrated_pictures = []
    for level in range(classes.shape[0]):
        onehot = (classes[level][None] == class_ids[:, None, None]).astype(jnp.float32)
        filters = jnp.einsum(
            "cfrk,cxy->frkxy", coefficients, onehot, precision=lax.Precision.HIGHEST
        )
        fields = extrapolate(fields, filters)
        partial_value = jnp.sum(fields[:, 0] * fields[:, 1], axis=(0, 1, 2))
        migrated_pictures.append(
            lax.psum_scatter(partial_value, "freq", scatter_dimension=0, tiled=True)
        )
    return jnp.stack(migrated_pictures)


def fits_lanes(records, classes, coefficients):
    tile_rows, width = records.shape[2:]
    height = classes.shape[1]
    class_count, group = coefficients.shape[:2]
    return (
        2 * group == SUBS
        and width == LANES
        and width // SUBS == SPACING
        and group * class_count <= LANES
        and height * group % LANES == 0
        and height // tile_rows % 2 == 0
        and 2 * (height * group // LANES) == tile_rows
    )


def per_device(records, wavelet, offsets, classes, coefficients):
    if fits_lanes(records, classes, coefficients):
        return fast_device(records, wavelet, offsets, classes, coefficients)
    return plain_device(records, wavelet, offsets, classes, coefficients)


def solution(mesh):
    placed = (
        P("parts", None, "freq", None),
        P("parts", None),
        P("parts", None, None, None),
        P("parts", None, None),
        P(None, "freq", None, None),
    )
    return jax.shard_map(
        per_device, mesh=mesh, in_specs=placed, out_specs=P("parts", "freq", None), check_vma=False
    )
```

profile of v0, /device:TPU:0, one launch (start us, length us, event | category | flops | bytes accessed | tf_op | source)
XLA Modules:
  0.0 92.2 jit_solution(3397652247856527128)
XLA Ops:
  0.0 0.0 copy-start
  0.0 0.0 copy-start.2
  0.0 0.0 copy-start.3
  0.0 0.0 copy-start.1
  0.0 0.0 copy-start.4
  0.0 1.9 %copy-done = bf16[1,1024,12,128]{3,1,2,0:T(8,128)(2,1)S(1)} copy-done((bf16[1,1024,12,128]{3,1,2,0:T(8,128)(2,1)S(1)}, bf16[1,1024,12,128]{3,1,2,0:T(8,128)(2,1)}, u32[]{:S(2)}) %copy-start) | copy-done | bytes 3145752
  1.9 2.4 %fusion.2 = f32[16,12,8,128]{3,2,1,0:T(8,128)} fusion(bf16[16,8,1024,1]{2,1,3,0:T(8,128)(2,1)} %constant.26, bf16[1,1024,12,128]{3,1,2,0:T(8,128)(2,1)S(1)} %copy-done), kind=kOutput, calls=%fused_computation.2 | convolution fusion | flops 402653184 | bytes 4194304 | tf_op jit(solution)/shard_map/jqt,txy->jxqy/dot_general | solution.py:325
  4.3 7.5 %all-to-all-start = ((f32[16,12,8,128]{3,2,1,0:T(8,128)}), f32[16,12,8,128]{3,2,1,0:T(8,128)}, u32[]{:S(2)}, u32[]{:S(2)}) async-start(f32[16,12,8,128]{3,2,1,0:T(8,128)} %fusion.2), calls=%async_computation | async-start | bytes 1572864 | tf_op jit(solution)/shard_map/all_to_all | solution.py:328
  11.8 0.0 copy-done.3
  11.8 0.6 pad.4.off_ref
  12.4 0.0 copy-done.2
  12.4 0.0 copy-done.1
  12.4 0.2 convolution_bitcast_fusion
  12.7 0.7 reshape.11.tab
  13.4 0.0 copy-done.4
  13.4 1.4 %fusion.6.wave_ref = f32[8]{0:T(128)} fusion(f32[16,8,1024]{2,1,0:T(8,128)} %constant.17.clone, s32[]{:T(128)S(6)} %select_n.4, f32[1024]{0:T(1024)S(1)} %bitcast.33), kind=kLoop, calls=%fused_computation.6 | loop fusion | flops 16376 | bytes 36900 | tf_op jit(solution)/shard_map/reduce_sum | solution.py:331
  14.8 29.0 %source_steps.1 = (f32[4,2,6,16,8,128]{5,4,3,2,1,0:T(8,128)}, s32[4,6,16,8,128]{4,3,2,1,0:T(8,128)}) custom-call(s32[2,8,128]{2,1,0:T(8,128)} %pad.4.off_ref, f32[8]{0:T(128)} %fusion.6.wave_ref, f32[2,9,128]{2,1,0:T(8,128)} %reshape.11.tab, s32[4,192,128]{2,1,0:T(8,128)} %classes.1), custom_call_target="tpu_custom_call" | custom-call | flops 1000000000 | bytes 60000000 | tf_op jit(solution)/shard_map/source_steps/pallas_call | solution.py:343
  43.8 0.0 all-to-all-done.received
  43.8 35.2 %receiver_steps.1 = f32[768,128]{1,0:T(8,128)} custom-call(f32[16,12,8,128]{3,2,1,0:T(8,128)} %all-to-all-done.received, f32[4,2,6,16,8,128]{5,4,3,2,1,0:T(8,128)} %get-tuple-element.7.src, f32[2,9,128]{2,1,0:T(8,128)} %reshape.11.tab, s32[4,6,16,8,128]{4,3,2,1,0:T(8,128)} %get-tuple-element.8.idx), custom_call_target="tpu_custom_call" | custom-call | flops 1000000000 | bytes 60000000 | tf_op jit(solution)/shard_map/receiver_steps/pallas_call | solution.py:358
  79.0 11.9 %exchange_tiles.1 = f32[12,4,128]{2,1,0:T(4,128)} custom-call(f32[2,8,48,128]{3,2,1,0:T(8,128)} %bitcast.30), custom_call_target="tpu_custom_call" | custom-call | tf_op jit(solution)/shard_map/exchange_tiles/pallas_call | solution.py:370
  90.9 1.3 %copy.30 = f32[4,12,128]{2,0,1:T(4,128)} copy(f32[4,12,128]{2,0,1:T(4,128)} %bitcast.31) | data formatting | bytes 49152
  (2 shorter events, 0.0 us)
Async XLA Ops:
  0.0 1.9 %copy-start = (bf16[1,1024,12,128]{3,1,2,0:T(8,128)(2,1)S(1)}, bf16[1,1024,12,128]{3,1,2,0:T(8,128)(2,1)}, u32[]{:S(2)}) copy-start(bf16[1,1024,12,128]{3,1,2,0:T(8,128)(2,1)} %param.7) | copy-start | bytes 9437188
  0.0 12.4 %copy-start.2 = (f32[9,9,1,1]{1,0,3,2:T(8,128)S(1)}, f32[9,9,1,1]{1,0,3,2:T(8,128)}, u32[]{:S(2)}) copy-start(f32[9,9,1,1]{1,0,3,2:T(8,128)} %constant.27) | copy-start | bytes 976
  0.0 11.8 %copy-start.3 = (s32[1,12,8,2]{1,3,2,0:T(2,128)S(1)}, s32[1,12,8,2]{1,3,2,0:T(2,128)}, u32[]{:S(2)}) copy-start(s32[1,12,8,2]{1,3,2,0:T(2,128)} %param.9) | copy-start | bytes 2308
  0.0 12.4 %copy-start.1 = (f32[32,4,2,9]{0,2,3,1:T(2,128)S(1)}, f32[32,4,2,9]{0,2,3,1:T(2,128)}, u32[]{:S(2)}) copy-start(f32[32,4,2,9]{0,2,3,1:T(2,128)} %param.11) | copy-start | bytes 27652
  0.0 13.3 %copy-start.4 = (f32[1,1024]{1,0:T(1,128)S(1)}, f32[1,1024]{1,0:T(1,128)}, u32[]{:S(2)}) copy-start(f32[1,1024]{1,0:T(1,128)} %param.8) | copy-start | bytes 12292
  4.3 39.5 %all-to-all-start = ((f32[16,12,8,128]{3,2,1,0:T(8,128)}), f32[16,12,8,128]{3,2,1,0:T(8,128)}, u32[]{:S(2)}, u32[]{:S(2)}) async-start(f32[16,12,8,128]{3,2,1,0:T(8,128)} %fusion.2), calls=%async_computation | async-start | bytes 1572864 | tf_op jit(solution)/shard_map/all_to_all | solution.py:328
where the time goes:
time: 92.6 us; the launch traced here: 92.2 us
  Pallas kernels  76.1 us (82%)
  starting transfers between devices  7.46 us (8%)
  local copies, waits for them, and re-layouts  4.58 us (5%)
  matrix products  2.61 us (3%)
  other arithmetic  1.41 us (2%)
    pallas_call x1, Pallas kernels, receive(): pl.pallas_call(functools.partial(receiver_kernel, group, begin, end - beg...  35.2 us
    pallas_call x1, Pallas kernels, fast_device(): pl.pallas_call(functools.partial(source_kernel, group, class_count), out_...  29 us
    pallas_call x1, Pallas kernels, fast_device(): pl.pallas_call(functools.partial(exchange_kernel, ranks), out_shape=jax.S...  11.9 us
    all_to_all x1, starting transfers between devices, fast_device(): lax.all_to_all(spectra, 'freq', split_axis=0, concat_axis=0, tiled=True)  7.46 us
    unnamed x12, local copies, waits for them, and re-layouts  3.25 us
    dot_general x1, matrix products, fast_device(): jnp.einsum('jqt,txy->jxqy', narrow, records[0], preferred_element_type=jn...  2.41 us
  transfers between devices with their start and end apart: 1, of which 0 were waited for; matrix products, arithmetic and copies ran while one was open for 3% of the time, Pallas kernels for 31%

commit v1 on v0

--- a/solution.py
+++ b/solution.py
@@ -209,106 +209,116 @@
     lax.fori_loop(1, depths, depth, 0)
 
 
-def receiver_kernel(group, begin, steps, received, src, tab, idx, out, acc, cur, flat, turned):
-    nx, ny = idx.shape[1:3]
+def exchange_peers(ranks):
+    me = lax.axis_index("freq")
+    return me, [lax.rem(me + k, ranks) for k in range(1, ranks)]
+
+
+def remote(src, dst, send, recv, peer):
+    return pltpu.make_async_remote_copy(
+        src_ref=src,
+        dst_ref=dst,
+        send_sem=send,
+        recv_sem=recv,
+        device_id={"freq": peer},
+        device_id_type=pl.DeviceIdType.MESH,
+    )
+
+
+def unpack_received(received, acc, flat, group, nx, ny):
+    senders = received.shape[0]
+    sub3 = lax.broadcasted_iota(jnp.int32, (senders, SUBS, LANES), 1)
+    upper = sub3 < group
+    for x in range(nx):
+        a, b = received[:, x], received[:, nx + x]
+        parts = (
+            jnp.where(upper, a, pltpu.roll(b, group, 1)),
+            jnp.where(upper, pltpu.roll(a, group, 1), b),
+        )
+        for r in range(2):
+            flat[r] = jnp.transpose(parts[r].reshape(LANES, LANES))
+            for y in range(ny):
+                acc[r, x, y] = flat[r, pl.ds(y, SUBS, stride=ny), :]
+
+
+def form_image(src, acc, flat, turned, image, group, nx, ny):
+    owners = image.shape[0] // 16
+    for x in range(nx):
+        for y in range(ny):
+            v = src[0, x, y] * acc[0, x, y] - src[1, x, y] * acc[1, x, y]
+            shift = 1
+            while shift < group:
+                v = v + pltpu.roll(v, shift, 1)
+                shift *= 2
+            flat[x % 2, pl.ds(y, SUBS, stride=ny), :] = v
+        turned[x % 2] = jnp.transpose(flat[x % 2])
+        for b in range(2):
+            lane = b * group + group - 1
+            image[pl.ds(b * nx + x, owners, stride=16), :] = (
+                turned[x % 2, pl.ds(lane, owners, stride=2 * group), :]
+            )
+
+
+def migrate_kernel(
+    group, class_count, ranks,
+    off_ref, wave_ref, tab, classes, spectra,
+    out,
+    src, idx, cur, acc, flat, turned, received, image, slots,
+    local_sem, a_send, a_recv, i_send, i_recv,
+):
+    depths, nx, ny = idx.shape[:3]
     degrees = tab.shape[1]
-    if begin == 0:
-        senders = received.shape[0]
-        sub3 = lax.broadcasted_iota(jnp.int32, (senders, SUBS, LANES), 1)
-        upper = sub3 < group
-        for x in range(nx):
-            a, b = received[:, x], received[:, nx + x]
-            parts = (
-                jnp.where(upper, a, pltpu.roll(b, group, 1)),
-                jnp.where(upper, pltpu.roll(a, group, 1), b),
-            )
-            for r in range(2):
-                flat[r] = jnp.transpose(parts[r].reshape(LANES, LANES))
-                for y in range(ny):
-                    acc[r, x, y] = flat[r, pl.ds(y, SUBS, stride=ny), :]
-    halves = 2
-    owners = LANES // (group * halves)
-    stride = out.shape[0] // owners
-
-    def depth(n, carry):
-        d = begin + n
-        field = received if begin else acc
-        degree_zero(
-            cur, acc, tab, idx.at[d], nx, ny, lambda x, y: (field[0, x, y], field[1, x, y])
-        )
-        all_degrees(cur, 2, acc, tab, idx.at[d], group, nx, ny, degrees)
-        for x in range(nx):
-            for y in range(ny):
-                v = src[d, 0, x, y] * acc[0, x, y] - src[d, 1, x, y] * acc[1, x, y]
-                shift = 1
-                while shift < group:
-                    v = v + pltpu.roll(v, shift, 1)
-                    shift *= 2
-                flat[x % 2, pl.ds(y, SUBS, stride=ny), :] = v
-            turned[x % 2] = jnp.transpose(flat[x % 2])
-            for b in range(halves):
-                at = (n * halves + b) * nx + x
-                for c in range(2):
-                    lane = (c * halves + b) * group + group - 1
-                    out[pl.ds(c * (owners // 2) * stride + at, owners // 2, stride=stride), :] = (
-                        turned[x % 2, pl.ds(lane, owners // 2, stride=2 * halves * group), :]
-                    )
-        return carry
-
-    if steps == 1:
-        depth(0, 0)
-    else:
-        lax.fori_loop(0, steps, depth, 0)
-
-
-def exchange_kernel(ranks, image, out, half, summed, slots, pair_sems, send_sem, recv_sem):
-    me = lax.axis_index("freq")
-    core, chip = lax.rem(me, 2), me // 2
-    other = chip * 2 + 1 - core
-    chips = ranks // 2
-    tile, depths = out.shape[:2]
-
-    def reach(k):
-        return lax.rem(chip + k, chips) * 2 + core
-
+    me, peers = exchange_peers(ranks)
     barrier = pltpu.get_barrier_semaphore()
-    for peer in [other] + [reach(k) for k in range(1, chips)]:
+    for peer in peers:
         pl.semaphore_signal(
             barrier, inc=1, device_id={"freq": peer}, device_id_type=pl.DeviceIdType.MESH
         )
-    pl.semaphore_wait(barrier, chips)
-    swap = pltpu.make_async_remote_copy(
-        src_ref=image.at[1 - core],
-        dst_ref=half,
-        send_sem=pair_sems.at[0],
-        recv_sem=pair_sems.at[1],
-        device_id={"freq": other},
-        device_id_type=pl.DeviceIdType.MESH,
-    )
-    swap.start()
-    swap.wait()
-    copies = []
-    for j in range(chips):
-        summed[j] = image[core, j] + half[j]
-    for k in range(1, chips):
-        copy = pltpu.make_async_remote_copy(
-            src_ref=summed.at[lax.rem(chip + k, chips)],
-            dst_ref=slots.at[k - 1],
-            send_sem=send_sem.at[k - 1],
-            recv_sem=recv_sem.at[k - 1],
-            device_id={"freq": reach(k)},
-            device_id_type=pl.DeviceIdType.MESH,
-        )
+    pl.semaphore_wait(barrier, ranks - 1)
+    own = pltpu.make_async_copy(spectra.at[me], received.at[me], local_sem)
+    own.start()
+    fields = []
+    for k, peer in enumerate(peers):
+        copy = remote(spectra.at[peer], received.at[me], a_send.at[k], a_recv.at[k], peer)
         copy.start()
-        copies.append(copy)
-    total = summed[chip]
-    for k in range(1, chips):
-        copies[k - 1].wait_recv()
-        total = total + slots[k - 1]
+        fields.append(copy)
+    source_kernel(group, class_count, off_ref, wave_ref, tab, classes, src, idx, cur, flat)
+    own.wait()
+    for copy in fields:
+        copy.wait()
+    unpack_received(received, acc, flat, group, nx, ny)
+
+    def sends(d):
+        return [
+            remote(
+                image.at[d, pl.ds(peer * 16, 16)],
+                slots.at[d, k],
+                i_send.at[d, k],
+                i_recv.at[d, k],
+                peer,
+            )
+            for k, peer in enumerate(peers)
+        ]
+
+    def depth(d, carry):
+        degree_zero(cur, acc, tab, idx.at[d], nx, ny, lambda x, y: (acc[0, x, y], acc[1, x, y]))
+        all_degrees(cur, 2, acc, tab, idx.at[d], group, nx, ny, degrees)
+        form_image(src.at[d], acc, flat, turned, image.at[d], group, nx, ny)
+        for copy in sends(d):
+            copy.start()
+        return carry
+
+    lax.fori_loop(0, depths, depth, 0)
+    tile = out.shape[1]
     for d in range(depths):
-        out[:, d, :] = total[d * tile : (d + 1) * tile]
-    for copy in copies:
-        copy.wait_send()
+        total = image[d, pl.ds(me * 16, 16), :]
+        for k, copy in enumerate(sends(d)):
+            copy.wait_recv()
+            total = total + slots[d, k]
+        out[d] = total[:tile]
+    for d in range(depths):
+        for copy in sends(d):
+            copy.wait_send()
 
 
 def fast_device(records, wavelet, offsets, classes, coefficients):
@@ -325,7 +335,6 @@
     spectra = jnp.einsum(
         "jqt,txy->jxqy", narrow, records[0], preferred_element_type=jnp.float32
     )
-    received = lax.all_to_all(spectra, "freq", split_axis=0, concat_axis=0, tiled=True)
 
     mine = lax.dynamic_index_in_dim(jnp.asarray(pair), lax.axis_index("freq"), 0, keepdims=False)
     wave = jnp.sum(mine * wavelet, axis=1)
@@ -340,50 +349,30 @@
     square = pltpu.VMEM((2, LANES, LANES), jnp.float32)
     vmem = pl.BlockSpec(memory_space=pltpu.VMEM)
     smem = pl.BlockSpec(memory_space=pltpu.SMEM)
-    source, index = pl.pallas_call(
-        functools.partial(source_kernel, group, class_count),
-        out_shape=[
-            jax.ShapeDtypeStruct((depths,) + plane, jnp.float32),
-            jax.ShapeDtypeStruct((depths,) + plane[1:], jnp.int32),
-        ],
-        in_specs=[vmem, smem, vmem, vmem],
-        out_specs=[vmem] * 2,
-        scratch_shapes=[pltpu.VMEM(plane, jnp.float32), square],
-        cost_estimate=pl.CostEstimate(flops=10**9, bytes_accessed=6 * 10**7, transcendentals=0),
-        name="source_steps",
-    )(off, wave, tab, classes)
-
-    def receive(begin, end, field):
-        rows = -(-(end - begin) * tile_rows // SUBS) * SUBS
-        return pl.pallas_call(
-            functools.partial(receiver_kernel, group, begin, end - begin),
-            out_shape=jax.ShapeDtypeStruct((ranks * rows, width), jnp.float32),
-            in_specs=[vmem] * 4,
-            out_specs=vmem,
-            scratch_shapes=[pltpu.VMEM(plane, jnp.float32)] * 2 + [square, square],
-            cost_estimate=pl.CostEstimate(flops=10**9, bytes_accessed=6 * 10**7, transcendentals=0),
-            name="receiver_steps",
-        )(field, source, tab, index)
-
-    image = receive(0, depths, received)
-    rows = image.shape[0] // ranks
-    tiles = pl.pallas_call(
-        functools.partial(exchange_kernel, ranks),
-        out_shape=jax.ShapeDtypeStruct((tile_rows, depths, width), jnp.float32),
-        in_specs=[vmem],
+    return pl.pallas_call(
+        functools.partial(migrate_kernel, group, class_count, ranks),
+        out_shape=jax.ShapeDtypeStruct((depths, tile_rows, width), jnp.float32),
+        in_specs=[vmem, smem, vmem, vmem, vmem],
         out_specs=vmem,
         scratch_shapes=[
-            pltpu.VMEM((ranks // 2, rows, width), jnp.float32),
-            pltpu.VMEM((ranks // 2, rows, width), jnp.float32),
-            pltpu.VMEM((ranks // 2 - 1, rows, width), jnp.float32),
-            pltpu.SemaphoreType.DMA((2,)),
-            pltpu.SemaphoreType.DMA((ranks // 2 - 1,)),
-            pltpu.SemaphoreType.DMA((ranks // 2 - 1,)),
+            pltpu.VMEM((depths,) + plane, jnp.float32),
+            pltpu.VMEM((depths,) + plane[1:], jnp.int32),
+            pltpu.VMEM(plane, jnp.float32),
+            pltpu.VMEM(plane, jnp.float32),
+            square,
+            square,
+            pltpu.VMEM(spectra.shape, jnp.float32),
+            pltpu.VMEM((depths, ranks * 16, width), jnp.float32),
+            pltpu.VMEM((depths, ranks - 1, 16, width), jnp.float32),
+            pltpu.SemaphoreType.DMA,
+            pltpu.SemaphoreType.DMA((ranks - 1,)),
+            pltpu.SemaphoreType.DMA((ranks - 1,)),
+            pltpu.SemaphoreType.DMA((depths, ranks - 1)),
+            pltpu.SemaphoreType.DMA((depths, ranks - 1)),
         ],
         compiler_params=pltpu.CompilerParams(collective_id=0, has_side_effects=True),
-        name="exchange_tiles",
-    )(image.reshape(2, ranks // 2, rows, width))
-    return tiles.transpose(1, 0, 2)
+        name="migrate",
+    )(off, wave, tab, classes, spectra)
 
 
 def dft_table(count, record_duration):

time: 92.6 us -> 76.6 us (0.83)
  Pallas kernels: 76.1 us -> 67.9 us
  starting transfers between devices: 7.46 us -> 0 us
  local copies, waits for them, and re-layouts: 4.58 us -> 3.4 us
    pallas_call x3 -> x1, Pallas kernels: 76.1 us -> 67.9 us  [fast_device(): pl.pallas_call(functools.partial(migrate_kernel, group, class_count, rank...]
    all_to_all x1 -> x0, starting transfers between devices: 7.46 us -> none  [fast_device(): lax.all_to_all(spectra, 'freq', split_axis=0, concat_axis=0, tiled=True)]
    unnamed x12 -> x3, local copies, waits for them, and re-layouts: 3.25 us -> 0.7 us
    pallas_call x0 -> x1, local copies, waits for them, and re-layouts: none -> 1.38 us  [fast_device(): pl.pallas_call(functools.partial(migrate_kernel, group, class_count, rank...]
  transfers between devices with their start and end apart: 1 -> 0, of which waited for: 0 -> 0; matrix products, arithmetic and copies ran while one was open for 3% -> 0% of each run, Pallas kernels for 31% -> 0%
where the time goes in v1:
time: 76.6 us; the launch traced here: 76.3 us
  Pallas kernels  67.9 us (89%)
  local copies, waits for them, and re-layouts  3.4 us (4%)
  matrix products  3.39 us (4%)
  other arithmetic  1.6 us (2%)
    pallas_call x1, Pallas kernels, fast_device(): pl.pallas_call(functools.partial(migrate_kernel, group, class_count, rank...  67.9 us
    dot_general x1, matrix products, fast_device(): jnp.einsum('jqt,txy->jxqy', narrow, records[0], preferred_element_type=jn...  2.41 us
    reduce_sum x1, other arithmetic, fast_device(): wave = jnp.sum(mine * wavelet, axis=1)  1.6 us

profile of v1, /device:TPU:0, one launch (start us, length us, event | category | flops | bytes accessed | tf_op | source)
XLA Modules:
  0.0 76.3 jit_solution(8790607171252744287)
XLA Ops:
  0.0 0.0 copy-start
  0.0 1.6 %fusion.6.wave_ref = f32[8]{0:T(128)} fusion(f32[16,8,1024]{2,1,0:T(8,128)} %constant.17.clone, s32[]{:T(128)S(6)} %select_n.4, f32[1024]{0:T(1024)} %bitcast.29), kind=kLoop, calls=%fused_computation.6 | loop fusion | flops 16376 | bytes 36900 | tf_op jit(solution)/shard_map/reduce_sum | solution.py:340
  1.6 0.7 copy.29
  2.3 0.6 pad.4.off_ref
  2.9 1.0 %convolution_bitcast_fusion = f32[2,9,4,32]{3,1,0,2:T(8,128)S(1)} fusion(f32[9,9,1,1]{1,0,3,2:T(8,128)} %constant.26, f32[32,4,2,9]{0,2,3,1:T(2,128)} %param.11), kind=kOutput, calls=%fused_computation.3 | convolution fusion | flops 248832 | bytes 18756 | tf_op jit(solution)/shard_map/jk,cfrk->rjfc/dot_general | solution.py:344
  3.9 0.7 reshape.7.tab
  4.6 0.0 copy-done
  4.6 2.4 %fusion.2.spectra = f32[16,12,8,128]{3,2,1,0:T(8,128)} fusion(bf16[16,8,1024,1]{2,1,3,0:T(8,128)(2,1)} %constant.27, bf16[1,1024,12,128]{3,1,2,0:T(8,128)(2,1)S(1)} %copy-done), kind=kOutput, calls=%fused_computation.2 | convolution fusion | flops 402653184 | bytes 4194304 | tf_op jit(solution)/shard_map/jqt,txy->jxqy/dot_general | solution.py:335
  7.0 67.9 %migrate.1 = f32[4,12,128]{2,1,0:T(8,128)} custom-call(s32[2,8,128]{2,1,0:T(8,128)} %pad.4.off_ref, f32[8]{0:T(128)} %fusion.6.wave_ref, f32[2,9,128]{2,1,0:T(8,128)} %reshape.7.tab, s32[4,192,128]{2,1,0:T(8,128)} %classes.1, f32[16,12,8,128]{3,2,1,0:T(8,128)} %fusion.2.spectra), custom_call_target="tpu_custom_call" | custom-call | tf_op jit(solution)/shard_map/migrate/pallas_call | solution.py:352
  74.9 1.4 %copy.21 = f32[4,12,128]{2,0,1:T(4,128)} copy(f32[4,12,128]{2,1,0:T(8,128)} %migrate.1) | data formatting | bytes 49152 | tf_op jit(solution)/shard_map/migrate/pallas_call | solution.py:352
  (1 shorter events, 0.0 us)
Async XLA Ops:
  0.0 4.6 %copy-start = (bf16[1,1024,12,128]{3,1,2,0:T(8,128)(2,1)S(1)}, bf16[1,1024,12,128]{3,1,2,0:T(8,128)(2,1)}, u32[]{:S(2)}) copy-start(bf16[1,1024,12,128]{3,1,2,0:T(8,128)(2,1)} %param.7) | copy-start | bytes 9437188

commit v2 on v1

--- a/solution.py
+++ b/solution.py
@@ -13,7 +13,8 @@
 SPACING = 16
 LANES = 128
 SUBS = 8
-NODES = (0.0, 1.0)
+VMEM_BYTES = 60 * 2**20
+NODES = (0.75, 1.0)
 
 
 first_bin = 4
@@ -32,7 +33,8 @@
     poly = np.polynomial.Polynomial
     basis = [poly([1.0])]
     for j in range(degrees - 1):
-        basis.append(basis[-1] * poly([-16.0 * NODES[j % 2], 16.0]))
+        node = NODES[j] if j < len(NODES) else 0.0
+        basis.append(basis[-1] * poly([-16.0 * node, 16.0]))
     matrix = np.zeros((degrees, degrees))
     for j, b in enumerate(basis):
         matrix[: len(b.coef), j] = b.coef
@@ -82,17 +84,24 @@
         rows = [classes[d, pl.ds(x, blocks, stride=nx), :] for d, x in some]
         slot = n // group % 2
         flat[slot] = jnp.transpose(jnp.concatenate(rows, axis=0).astype(jnp.float32))
-        for y in range(ny):
-            line = flat[slot, pl.ds(y, SUBS, stride=ny), :].astype(jnp.int32)
-            for i, (d, x) in enumerate(some):
+        for i, (d, x) in enumerate(some):
+            for y in range(ny):
+                line = flat[slot, pl.ds(y, SUBS, stride=ny), :].astype(jnp.int32)
                 idx[d, x, y] = pick(line, lane // group + i * blocks) + lane % group * class_count
 
 
-def degree_pass(cur, planes, acc, tab, k, idx, node, group, nx, ny):
+def look_up(tab, idx, filters, x, y):
+    degrees = tab.shape[1]
+    place = idx[x, y]
+    for k in range(degrees):
+        for part in range(2):
+            filters[k, part, x, y] = pick(row_of(tab, part, k), place)
+
+
+def degree_pass(cur, planes, acc, filters, node, group, nx, ny, beside):
     lane, sub = iotas()
     low, high = lane >= group, lane < LANES - group
     first, last = sub >= 1, sub < SUBS - 1
-    gr, gi = row_of(tab, 0, k), row_of(tab, 1, k)
 
     def along_x(c, y):
         v = [cur[c, x, y] for x in range(nx)]
@@ -119,14 +128,14 @@
                 nxt = [jnp.where(last, pltpu.roll(e, SUBS - 1, 0), 0.0) for e in u_first[c]]
             q_next = [a + b for a, b in zip(u[c], nxt)]
             total = [a + b for a, b in zip(q[c], q_next)]
-            if node:
-                total = [t - (16.0 * node) * cur[c, x, y] for x, t in enumerate(total)]
+            if node is not None:
+                total = [t - node * cur[c, x, y] for x, t in enumerate(total)]
             for x in range(nx):
                 cur[c, x, y] = total[x]
             made.append(total)
             u[c], q[c] = nxt, q_next
         for x in range(nx):
-            hr, hi = pick(gr, idx[x, y]), pick(gi, idx[x, y])
+            hr, hi = filters[0, x, y], filters[1, x, y]
             if planes == 2:
                 re, im = made[0][x], made[1][x]
                 acc[0, x, y] = acc[0, x, y] + (hr * re - hi * im)
@@ -134,28 +143,38 @@
             else:
                 acc[0, x, y] = acc[0, x, y] + hr * made[0][x]
                 acc[1, x, y] = acc[1, x, y] + hi * made[0][x]
-
-
-def all_degrees(cur, planes, acc, tab, idx, group, nx, ny, degrees):
-    def two(j, carry):
-        degree_pass(cur, planes, acc, tab, 2 * j + 1, idx, NODES[0], group, nx, ny)
-        degree_pass(cur, planes, acc, tab, 2 * j + 2, idx, NODES[1], group, nx, ny)
-        return carry
-
-    lax.fori_loop(0, (degrees - 1) // 2, two, 0)
-    if degrees % 2 == 0:
-        degree_pass(cur, planes, acc, tab, degrees - 1, idx, NODES[0], group, nx, ny)
-
-
-def degree_zero(cur, acc, tab, idx, nx, ny, load):
-    gr, gi = row_of(tab, 0, 0), row_of(tab, 1, 0)
-
+        beside(y)
+
+
+def all_degrees(cur, planes, acc, filters, group, nx, ny, ahead=None):
+    steps = filters.shape[0] - 1
+    share = nx * ny // steps
+
+    def one(shifted, j, carry):
+        def beside(y):
+            if ahead is not None:
+                for n in range(share * y // ny, share * (y + 1) // ny):
+                    ahead(n % nx, j * (share // nx) + n // nx)
+
+        node = None
+        if shifted:
+            node = jnp.float32(16.0 * NODES[-1])
+            for n, value in enumerate(NODES[:-1]):
+                node = jnp.where(j == n, jnp.float32(16.0 * value), node)
+        degree_pass(cur, planes, acc, filters.at[j + 1], node, group, nx, ny, beside)
+        return carry
+
+    lax.fori_loop(0, len(NODES), functools.partial(one, True), 0)
+    lax.fori_loop(len(NODES), steps, functools.partial(one, False), 0)
+
+
+def degree_zero(cur, acc, filters, nx, ny, load):
     def row(y, carry):
         for x in range(nx):
             re, im = load(x, y)
             cur[0, x, y] = re
             cur[1, x, y] = im
-            hr, hi = pick(gr, idx[x, y]), pick(gi, idx[x, y])
+            hr, hi = filters[0, 0, x, y], filters[0, 1, x, y]
             acc[0, x, y] = hr * re - hi * im
             acc[1, x, y] = hr * im + hi * re
         return carry
@@ -163,12 +182,16 @@
     lax.fori_loop(0, ny, row, 0, unroll=2)
 
 
-def source_kernel(group, class_count, off_ref, wave_ref, tab, classes, out, idx, cur, flat):
+def source_steps(group, off_ref, wave_ref, tab, out, idx, filters, cur):
     depths, nx, ny = idx.shape[:3]
-    degrees = tab.shape[1]
     lane, _ = iotas()
-    lane_classes(classes, idx, flat, group, class_count)
-    gr, gi = row_of(tab, 0, 0), row_of(tab, 1, 0)
+
+    def first(y, carry):
+        for x in range(nx):
+            look_up(tab, idx.at[0], filters.at[0], x, y)
+        return carry
+
+    lax.fori_loop(0, ny, first, 0)
     row_x = [lane // group * nx + x for x in range(nx)]
     off_x = [pick(off_ref[0], r // SPACING) for r in row_x]
     off_y = [pick(off_ref[1], r // SPACING) for r in row_x]
@@ -178,12 +201,16 @@
             hit = (row_x[x] % SPACING == off_x[x]) & (off_y[x] == y)
             v = jnp.where(hit, 1.0, 0.0)
             cur[0, x, y] = v
-            out[0, 0, x, y] = pick(gr, idx[0, x, y]) * v
-            out[0, 1, x, y] = pick(gi, idx[0, x, y]) * v
+            out[0, 0, x, y] = filters[0, 0, 0, x, y] * v
+            out[0, 1, x, y] = filters[0, 0, 1, x, y] * v
         return carry
 
     lax.fori_loop(0, ny, spike_row, 0, unroll=2)
-    all_degrees(cur, 1, out.at[0], tab, idx.at[0], group, nx, ny, degrees)
+
+    def ahead_of(d):
+        return functools.partial(look_up, tab, idx.at[d], filters.at[d])
+
+    all_degrees(cur, 1, out.at[0], filters.at[0], group, nx, ny, ahead_of(1))
     wr, wi = jnp.zeros((SUBS, LANES), jnp.float32), jnp.zeros((SUBS, LANES), jnp.float32)
     for f in range(group):
         wr = jnp.where(lane % group == f, wave_ref[f], wr)
@@ -199,14 +226,16 @@
     lax.fori_loop(0, ny, wave_row, 0, unroll=2)
 
     def depth(d, carry):
-        def load(x, y):
-            return out[d - 1, 0, x, y], out[d - 1, 1, x, y]
-
-        degree_zero(cur, out.at[d], tab, idx.at[d], nx, ny, load)
-        all_degrees(cur, 2, out.at[d], tab, idx.at[d], group, nx, ny, degrees)
-        return carry
-
-    lax.fori_loop(1, depths, depth, 0)
+        filter_step(group, cur, out.at[d - 1], out.at[d], filters.at[d], ahead_of(d + 1))
+        return carry
+
+    lax.fori_loop(1, depths - 1, depth, 0)
+
+
+def filter_step(group, cur, begin, end, filters, ahead=None):
+    nx, ny = begin.shape[1:3]
+    degree_zero(cur, end, filters, nx, ny, lambda x, y: (begin[0, x, y], begin[1, x, y]))
+    all_degrees(cur, 2, end, filters, group, nx, ny, ahead)
 
 
 def exchange_peers(ranks):
@@ -263,11 +292,10 @@
     group, class_count, ranks,
     off_ref, wave_ref, tab, classes, spectra,
     out,
-    src, idx, cur, acc, flat, turned, received, image, slots,
+    fields, idx, filters, cur, flat, turned, received, image, slots,
     local_sem, a_send, a_recv, i_send, i_recv,
 ):
     depths, nx, ny = idx.shape[:3]
-    degrees = tab.shape[1]
     me, peers = exchange_peers(ranks)
     barrier = pltpu.get_barrier_semaphore()
     for peer in peers:
@@ -277,17 +305,15 @@
     pl.semaphore_wait(barrier, ranks - 1)
     own = pltpu.make_async_copy(spectra.at[me], received.at[me], local_sem)
     own.start()
-    fields = []
-    for k, peer in enumerate(peers):
-        copy = remote(spectra.at[peer], received.at[me], a_send.at[k], a_recv.at[k], peer)
+    spread = [
+        remote(spectra.at[peer], received.at[me], a_send.at[k], a_recv.at[k], peer)
+        for k, peer in enumerate(peers)
+    ]
+    for copy in spread:
         copy.start()
-        fields.append(copy)
-    source_kernel(group, class_count, off_ref, wave_ref, tab, classes, src, idx, cur, flat)
-    own.wait()
-    for copy in fields:
-        copy.wait()
-    unpack_received(received, acc, flat, group, nx, ny)
-
+    lane_classes(classes, idx, flat, group, class_count)
+    source_steps(group, off_ref, wave_ref, tab, fields, idx, filters, cur)
+    acc = fields.at[depths]
     def sends(d):
         return [
             remote(
@@ -300,15 +326,29 @@
             for k, peer in enumerate(peers)
         ]
 
-    def depth(d, carry):
-        degree_zero(cur, acc, tab, idx.at[d], nx, ny, lambda x, y: (acc[0, x, y], acc[1, x, y]))
-        all_degrees(cur, 2, acc, tab, idx.at[d], group, nx, ny, degrees)
-        form_image(src.at[d], acc, flat, turned, image.at[d], group, nx, ny)
-        for copy in sends(d):
-            copy.start()
-        return carry
-
-    lax.fori_loop(0, depths, depth, 0)
+    def step(n, carry):
+        @pl.when(n == 1)
+        def _():
+            own.wait()
+            for copy in spread:
+                copy.wait()
+            unpack_received(received, acc, flat, group, nx, ny)
+
+        ready = jnp.minimum(n, 1)
+        begin = (depths - 2) * (1 - ready) + depths * ready
+        end = depths - 1 + ready
+        d = (depths - 1) * (1 - ready) + (n - 1) * ready
+        filter_step(group, cur, fields.at[begin], fields.at[end], filters.at[d])
+
+        @pl.when(n >= 1)
+        def _():
+            form_image(fields.at[d], acc, flat, turned, image.at[d], group, nx, ny)
+            for copy in sends(d):
+                copy.start()
+
+        return carry
+
+    lax.fori_loop(0, depths + 1, step, 0)
     tile = out.shape[1]
     for d in range(depths):
         total = image[d, pl.ds(me * 16, 16), :]
@@ -355,9 +395,9 @@
         in_specs=[vmem, smem, vmem, vmem, vmem],
         out_specs=vmem,
         scratch_shapes=[
-            pltpu.VMEM((depths,) + plane, jnp.float32),
+            pltpu.VMEM((depths + 1,) + plane, jnp.float32),
             pltpu.VMEM((depths,) + plane[1:], jnp.int32),
-            pltpu.VMEM(plane, jnp.float32),
+            pltpu.VMEM((depths, degrees) + plane, jnp.float32),
             pltpu.VMEM(plane, jnp.float32),
             square,
             square,
@@ -370,7 +410,9 @@
             pltpu.SemaphoreType.DMA((depths, ranks - 1)),
             pltpu.SemaphoreType.DMA((depths, ranks - 1)),
         ],
-        compiler_params=pltpu.CompilerParams(collective_id=0, has_side_effects=True),
+        compiler_params=pltpu.CompilerParams(
+            collective_id=0, has_side_effects=True, vmem_limit_bytes=VMEM_BYTES
+        ),
         name="migrate",
     )(off, wave, tab, classes, spectra)
 

time: 76.6 us -> 59.1 us (0.77)
  Pallas kernels: 67.9 us -> 50.4 us
    pallas_call x1, Pallas kernels: 67.9 us -> 50.4 us  [fast_device(): pl.pallas_call(functools.partial(migrate_kernel, group, class_count, rank...]
where the time goes in v2:
time: 59.1 us; the launch traced here: 58.8 us
  Pallas kernels  50.4 us (85%)
  local copies, waits for them, and re-layouts  3.4 us (6%)
  matrix products  3.39 us (6%)
  other arithmetic  1.6 us (3%)
    pallas_call x1, Pallas kernels, fast_device(): pl.pallas_call(functools.partial(migrate_kernel, group, class_count, rank...  50.4 us
    dot_general x1, matrix products, fast_device(): jnp.einsum('jqt,txy->jxqy', narrow, records[0], preferred_element_type=jn...  2.41 us
    reduce_sum x1, other arithmetic, fast_device(): wave = jnp.sum(mine * wavelet, axis=1)  1.6 us
    pallas_call x1, local copies, waits for them, and re-layouts, fast_device(): pl.pallas_call(functools.partial(migrate_kernel, group, class_count, rank...  1.38 us

profile of v2, /device:TPU:0, one launch (start us, length us, event | category | flops | bytes accessed | tf_op | source)
XLA Modules:
  0.0 58.8 jit_solution(7797031948256990328)
XLA Ops:
  0.0 0.0 copy-start
  0.0 1.6 %fusion.6.wave_ref = f32[8]{0:T(128)} fusion(f32[16,8,1024]{2,1,0:T(8,128)} %constant.17.clone, s32[]{:T(128)S(6)} %select_n.4, f32[1024]{0:T(1024)} %bitcast.29), kind=kLoop, calls=%fused_computation.6 | loop fusion | flops 16376 | bytes 36900 | tf_op jit(solution)/shard_map/reduce_sum | solution.py:380
  1.6 0.7 %copy.29 = s32[1,12,8,2]{1,2,3,0:T(8,128)S(1)} copy(s32[1,12,8,2]{1,3,2,0:T(2,128)} %param.9) | data formatting | bytes 1536 | tf_op args[2]
  2.3 0.6 %pad.4.off_ref = s32[2,8,128]{2,1,0:T(8,128)} pad(s32[2,8,12]{2,1,0:T(8,128)S(1)} %bitcast.28, s32[]{:T(128)} %constant.6.clone.1), padding=0_0x0_0x0_116 | pad | bytes 8964 | tf_op jit(solution)/shard_map/jit(_pad)/pad | solution.py:382
  2.9 1.0 %convolution_bitcast_fusion = f32[2,9,4,32]{3,1,0,2:T(8,128)S(1)} fusion(f32[9,9,1,1]{1,0,3,2:T(8,128)} %constant.26, f32[32,4,2,9]{0,2,3,1:T(2,128)} %param.11), kind=kOutput, calls=%fused_computation.3 | convolution fusion | flops 248832 | bytes 18756 | tf_op jit(solution)/shard_map/jk,cfrk->rjfc/dot_general | solution.py:384
  3.9 0.7 %reshape.7.tab = f32[2,9,128]{2,1,0:T(8,128)} reshape(f32[2,9,4,32]{3,2,1,0:T(4,128)S(1)} %copy.24) | data formatting | bytes 18432 | tf_op jit(solution)/shard_map/reshape | solution.py:385
  4.6 0.0 copy-done
  4.6 2.4 %fusion.2.spectra = f32[16,12,8,128]{3,2,1,0:T(8,128)} fusion(bf16[16,8,1024,1]{2,1,3,0:T(8,128)(2,1)} %constant.27, bf16[1,1024,12,128]{3,1,2,0:T(8,128)(2,1)S(1)} %copy-done), kind=kOutput, calls=%fused_computation.2 | convolution fusion | flops 402653184 | bytes 4194304 | tf_op jit(solution)/shard_map/jqt,txy->jxqy/dot_general | solution.py:375
  7.0 50.4 %migrate.1 = f32[4,12,128]{2,1,0:T(8,128)} custom-call(s32[2,8,128]{2,1,0:T(8,128)} %pad.4.off_ref, f32[8]{0:T(128)} %fusion.6.wave_ref, f32[2,9,128]{2,1,0:T(8,128)} %reshape.7.tab, s32[4,192,128]{2,1,0:T(8,128)} %classes.1, f32[16,12,8,128]{3,2,1,0:T(8,128)} %fusion.2.spectra), custom_call_target="tpu_custom_call" | custom-call | tf_op jit(solution)/shard_map/migrate/pallas_call | solution.py:392
  57.4 1.4 %copy.21 = f32[4,12,128]{2,0,1:T(4,128)} copy(f32[4,12,128]{2,1,0:T(8,128)} %migrate.1) | data formatting | bytes 49152 | tf_op jit(solution)/shard_map/migrate/pallas_call | solution.py:392
  (1 shorter events, 0.0 us)
Async XLA Ops:
  0.0 4.6 %copy-start = (bf16[1,1024,12,128]{3,1,2,0:T(8,128)(2,1)S(1)}, bf16[1,1024,12,128]{3,1,2,0:T(8,128)(2,1)}, u32[]{:S(2)}) copy-start(bf16[1,1024,12,128]{3,1,2,0:T(8,128)(2,1)} %param.7) | copy-start | bytes 9437188

commit v3 on v2

--- a/solution.py
+++ b/solution.py
@@ -71,7 +71,7 @@
 
 
 def row_of(tab, part, k):
-    return jnp.broadcast_to(tab[part, pl.ds(k, 1), :], (SUBS, LANES))
+    return jnp.broadcast_to(tab[k, pl.ds(part, 1), :], (SUBS, LANES))
 
 
 def lane_classes(classes, idx, flat, group, class_count):
@@ -91,20 +91,20 @@
 
 
 def look_up(tab, idx, filters, x, y):
-    degrees = tab.shape[1]
+    degrees = tab.shape[0]
     place = idx[x, y]
     for k in range(degrees):
         for part in range(2):
             filters[k, part, x, y] = pick(row_of(tab, part, k), place)
 
 
-def degree_pass(cur, planes, acc, filters, node, group, nx, ny, beside):
+def degree_pass(old, cur, planes, acc, filters, node, group, nx, ny, begin=None, beside=None):
     lane, sub = iotas()
     low, high = lane >= group, lane < LANES - group
     first, last = sub >= 1, sub < SUBS - 1
 
     def along_x(c, y):
-        v = [cur[c, x, y] for x in range(nx)]
+        v = [old[c, x, y] for x in range(nx)]
         before = jnp.where(low, pltpu.roll(v[nx - 1], group, 1), 0.0)
         after = jnp.where(high, pltpu.roll(v[0], LANES - group, 1), 0.0)
         ext = [before] + v + [after]
@@ -120,7 +120,7 @@
         u_first.append(start)
         q.append([a + b for a, b in zip(prev, start)])
     for y in range(ny):
-        made = []
+        made, was = [], []
         for c in range(planes):
             if y < ny - 1:
                 nxt = along_x(c, y + 1)
@@ -129,7 +129,9 @@
             q_next = [a + b for a, b in zip(u[c], nxt)]
             total = [a + b for a, b in zip(q[c], q_next)]
             if node is not None:
-                total = [t - node * cur[c, x, y] for x, t in enumerate(total)]
+                held = [old[c, x, y] for x in range(nx)]
+                total = [t - node * h for t, h in zip(total, held)]
+                was.append(held)
             for x in range(nx):
                 cur[c, x, y] = total[x]
             made.append(total)
@@ -138,60 +140,68 @@
             hr, hi = filters[0, x, y], filters[1, x, y]
             if planes == 2:
                 re, im = made[0][x], made[1][x]
-                acc[0, x, y] = acc[0, x, y] + (hr * re - hi * im)
-                acc[1, x, y] = acc[1, x, y] + (hr * im + hi * re)
+                if begin is None:
+                    acc[0, x, y] = acc[0, x, y] + (hr * re - hi * im)
+                    acc[1, x, y] = acc[1, x, y] + (hr * im + hi * re)
+                else:
+                    gr, gi = begin[0, x, y], begin[1, x, y]
+                    was_re, was_im = was[0][x], was[1][x]
+                    acc[0, x, y] = (gr * was_re - gi * was_im) + (hr * re - hi * im)
+                    acc[1, x, y] = (gr * was_im + gi * was_re) + (hr * im + hi * re)
             else:
                 acc[0, x, y] = acc[0, x, y] + hr * made[0][x]
                 acc[1, x, y] = acc[1, x, y] + hi * made[0][x]
-        beside(y)
-
-
-def all_degrees(cur, planes, acc, filters, group, nx, ny, ahead=None):
+        if beside is not None:
+            beside(y)
+
+
+def node_at(j):
+    node = jnp.float32(16.0 * NODES[-1])
+    for n, value in enumerate(NODES[:-1]):
+        node = jnp.where(j == n, jnp.float32(16.0 * value), node)
+    return node
+
+
+def spread_ahead(ahead, steps, j, nx, ny):
+    if ahead is None:
+        return None
+    share = nx * ny // steps
+
+    def beside(y):
+        for n in range(share * y // ny, share * (y + 1) // ny):
+            ahead(n % nx, j * (share // nx) + n // nx)
+
+    return beside
+
+
+def all_degrees(cur, planes, acc, filters, group, nx, ny, ahead=None, begin=None):
     steps = filters.shape[0] - 1
-    share = nx * ny // steps
+    done = 0
+    if begin is not None:
+        degree_pass(
+            begin, cur, planes, acc, filters.at[1], 16.0 * NODES[0], group, nx, ny,
+            filters.at[0], spread_ahead(ahead, steps, 0, nx, ny),
+        )
+        done = 1
 
     def one(shifted, j, carry):
-        def beside(y):
-            if ahead is not None:
-                for n in range(share * y // ny, share * (y + 1) // ny):
-                    ahead(n % nx, j * (share // nx) + n // nx)
-
-        node = None
-        if shifted:
-            node = jnp.float32(16.0 * NODES[-1])
-            for n, value in enumerate(NODES[:-1]):
-                node = jnp.where(j == n, jnp.float32(16.0 * value), node)
-        degree_pass(cur, planes, acc, filters.at[j + 1], node, group, nx, ny, beside)
+        degree_pass(
+            cur, cur, planes, acc, filters.at[j + 1], node_at(j) if shifted else None,
+            group, nx, ny, None, spread_ahead(ahead, steps, j, nx, ny),
+        )
         return carry
 
-    lax.fori_loop(0, len(NODES), functools.partial(one, True), 0)
+    if len(NODES) - done == 1:
+        one(True, done, 0)
+    else:
+        lax.fori_loop(done, len(NODES), functools.partial(one, True), 0)
     lax.fori_loop(len(NODES), steps, functools.partial(one, False), 0)
 
 
-def degree_zero(cur, acc, filters, nx, ny, load):
-    def row(y, carry):
-        for x in range(nx):
-            re, im = load(x, y)
-            cur[0, x, y] = re
-            cur[1, x, y] = im
-            hr, hi = filters[0, 0, x, y], filters[0, 1, x, y]
-            acc[0, x, y] = hr * re - hi * im
-            acc[1, x, y] = hr * im + hi * re
-        return carry
-
-    lax.fori_loop(0, ny, row, 0, unroll=2)
-
-
-def source_steps(group, off_ref, wave_ref, tab, out, idx, filters, cur):
+def source_steps(group, off_ref, wave, tab, out, idx, filters, cur):
     depths, nx, ny = idx.shape[:3]
     lane, _ = iotas()
 
-    def first(y, carry):
-        for x in range(nx):
-            look_up(tab, idx.at[0], filters.at[0], x, y)
-        return carry
-
-    lax.fori_loop(0, ny, first, 0)
     row_x = [lane // group * nx + x for x in range(nx)]
     off_x = [pick(off_ref[0], r // SPACING) for r in row_x]
     off_y = [pick(off_ref[1], r // SPACING) for r in row_x]
@@ -213,8 +223,10 @@
     all_degrees(cur, 1, out.at[0], filters.at[0], group, nx, ny, ahead_of(1))
     wr, wi = jnp.zeros((SUBS, LANES), jnp.float32), jnp.zeros((SUBS, LANES), jnp.float32)
     for f in range(group):
-        wr = jnp.where(lane % group == f, wave_ref[f], wr)
-        wi = jnp.where(lane % group == f, -wave_ref[group + f], wi)
+        wr = jnp.where(lane % group == f, jnp.broadcast_to(wave[pl.ds(f, 1), :], wr.shape), wr)
+        wi = jnp.where(
+            lane % group == f, -jnp.broadcast_to(wave[pl.ds(group + f, 1), :], wi.shape), wi
+        )
 
     def wave_row(y, carry):
         for x in range(nx):
@@ -234,8 +246,36 @@
 
 def filter_step(group, cur, begin, end, filters, ahead=None):
     nx, ny = begin.shape[1:3]
-    degree_zero(cur, end, filters, nx, ny, lambda x, y: (begin[0, x, y], begin[1, x, y]))
-    all_degrees(cur, 2, end, filters, group, nx, ny, ahead)
+    all_degrees(cur, 2, end, filters, group, nx, ny, ahead, begin)
+
+
+def small_tables(offsets, wavelet, coefs, off, wave, tab, wide, moments):
+    group, degrees, _, class_count = coefs.shape
+    rows, columns = offsets.shape[0], offsets.shape[2]
+    for by in range(rows):
+        for c in range(2):
+            off[c, pl.ds(by, 1), pl.ds(0, columns)] = offsets[by, pl.ds(c, 1), :]
+    wave[...] = jnp.broadcast_to(
+        jnp.sum(moments[...] * wavelet[...], axis=1, keepdims=True), wave.shape
+    )
+    wide[...] = jnp.zeros_like(wide)
+    for f in range(group):
+        for k in range(degrees):
+            wide[f, k, pl.ds(0, 2), pl.ds(0, class_count)] = coefs[f, k]
+    joined = []
+    for k in range(degrees):
+        row = wide[0, k]
+        for f in range(1, group):
+            row = row + pltpu.roll(wide[f, k], f * class_count, 1)
+        joined.append(row)
+    change = basis_change(degrees)
+    for j in range(degrees):
+        total = None
+        for k in range(degrees):
+            if change[j, k] != 0.0:
+                term = np.float32(change[j, k]) * joined[k]
+                total = term if total is None else total + term
+        tab[j] = total
 
 
 def exchange_peers(ranks):
@@ -275,45 +315,87 @@
     for x in range(nx):
         for y in range(ny):
             v = src[0, x, y] * acc[0, x, y] - src[1, x, y] * acc[1, x, y]
-            shift = 1
-            while shift < group:
-                v = v + pltpu.roll(v, shift, 1)
-                shift *= 2
             flat[x % 2, pl.ds(y, SUBS, stride=ny), :] = v
         turned[x % 2] = jnp.transpose(flat[x % 2])
         for b in range(2):
-            lane = b * group + group - 1
-            image[pl.ds(b * nx + x, owners, stride=16), :] = (
-                turned[x % 2, pl.ds(lane, owners, stride=2 * group), :]
-            )
+            total = turned[x % 2, pl.ds(b * group, owners, stride=2 * group), :]
+            for f in range(1, group):
+                total = total + turned[x % 2, pl.ds(b * group + f, owners, stride=2 * group), :]
+            image[pl.ds(b * nx + x, owners, stride=16), :] = total
 
 
 def migrate_kernel(
     group, class_count, ranks,
-    off_ref, wave_ref, tab, classes, spectra,
+    records, table, moments_all, wavelet, offsets, coefs, classes,
     out,
     fields, idx, filters, cur, flat, turned, received, image, slots,
-    local_sem, a_send, a_recv, i_send, i_recv,
+    traces, spectra, moments, off, wave, wide, tab,
+    local_sem, rec_sem, a_send, a_recv, i_send, i_recv,
 ):
     depths, nx, ny = idx.shape[:3]
+    tile = records.shape[0]
+    halves, pairs = 2, tile // 4
     me, peers = exchange_peers(ranks)
     barrier = pltpu.get_barrier_semaphore()
     for peer in peers:
         pl.semaphore_signal(
             barrier, inc=1, device_id={"freq": peer}, device_id_type=pl.DeviceIdType.MESH
         )
+    mine = pltpu.make_async_copy(moments_all.at[me], moments, local_sem)
+    mine.start()
+
+    def load(p):
+        rows = pl.ds(2 * p, 2)
+        return pltpu.make_async_copy(records.at[rows], traces.at[rows], rec_sem.at[p])
+
+    for p in range(halves * pairs):
+        load(p).start()
+    mine.wait()
+    small_tables(offsets, wavelet, coefs, off, wave, tab, wide, moments)
+    lane_classes(classes, idx, flat, group, class_count)
     pl.semaphore_wait(barrier, ranks - 1)
+
+    def spread(half):
+        rows = pl.ds(half * 2 * pairs, 2 * pairs)
+        return [
+            remote(
+                spectra.at[peer, rows],
+                received.at[me, rows],
+                a_send.at[half, k],
+                a_recv.at[half, k],
+                peer,
+            )
+            for k, peer in enumerate(peers)
+        ]
+
+    def transform(half, carry):
+        def pair(i, carry):
+            p = half * pairs + i
+            load(p).wait()
+            both = jnp.concatenate([traces[2 * p], traces[2 * p + 1]], axis=1)
+            made = jnp.dot(table[...], both, preferred_element_type=jnp.float32)
+            width = made.shape[1] // 2
+            for n in range(2):
+                spectra[:, 2 * p + n] = made[:, n * width : (n + 1) * width].reshape(
+                    ranks, SUBS, width
+                )
+            share = nx * ny // (halves * pairs)
+            for n in range(share):
+                at = p * share + n
+                look_up(tab, idx.at[0], filters.at[0], at // ny, at % ny)
+            return carry
+
+        lax.fori_loop(0, pairs, pair, 0)
+        for copy in spread(half):
+            copy.start()
+        return carry
+
+    lax.fori_loop(0, halves, transform, 0)
     own = pltpu.make_async_copy(spectra.at[me], received.at[me], local_sem)
     own.start()
-    spread = [
-        remote(spectra.at[peer], received.at[me], a_send.at[k], a_recv.at[k], peer)
-        for k, peer in enumerate(peers)
-    ]
-    for copy in spread:
-        copy.start()
-    lane_classes(classes, idx, flat, group, class_count)
-    source_steps(group, off_ref, wave_ref, tab, fields, idx, filters, cur)
+    source_steps(group, off, wave, tab, fields, idx, filters, cur)
     acc = fields.at[depths]
+
     def sends(d):
         return [
             remote(
@@ -330,8 +412,9 @@
         @pl.when(n == 1)
         def _():
             own.wait()
-            for copy in spread:
-                copy.wait()
+            for half in range(halves):
+                for copy in spread(half):
+                    copy.wait()
             unpack_received(received, acc, flat, group, nx, ny)
 
         ready = jnp.minimum(n, 1)
@@ -349,7 +432,6 @@
         return carry
 
     lax.fori_loop(0, depths + 1, step, 0)
-    tile = out.shape[1]
     for d in range(depths):
         total = image[d, pl.ds(me * 16, 16), :]
         for k, copy in enumerate(sends(d)):
@@ -371,28 +453,15 @@
     pair = np.stack(
         [cos_rows.reshape(ranks, group, -1), -sin_rows.reshape(ranks, group, -1)], axis=1
     ).reshape(ranks, 2 * group, record_duration)
-    narrow = jnp.asarray(pair).astype(jnp.bfloat16)
-    spectra = jnp.einsum(
-        "jqt,txy->jxqy", narrow, records[0], preferred_element_type=jnp.float32
-    )
-
-    mine = lax.dynamic_index_in_dim(jnp.asarray(pair), lax.axis_index("freq"), 0, keepdims=False)
-    wave = jnp.sum(mine * wavelet, axis=1)
-    off = offsets[0].transpose(2, 1, 0)
-    off = jnp.pad(off, ((0, 0), (0, 0), (0, LANES - off.shape[2])))
-    change = jnp.asarray(basis_change(degrees), jnp.float32)
-    tab = jnp.einsum("jk,cfrk->rjfc", change, coefficients, precision=lax.Precision.HIGHEST)
-    tab = tab.reshape(2, degrees, group * class_count)
-    tab = jnp.pad(tab, ((0, 0), (0, 0), (0, LANES - group * class_count)))
-
+    narrow = jnp.asarray(pair.reshape(2 * NF, record_duration)).astype(jnp.bfloat16)
     plane = (2, nx, ny, SUBS, LANES)
     square = pltpu.VMEM((2, LANES, LANES), jnp.float32)
     vmem = pl.BlockSpec(memory_space=pltpu.VMEM)
-    smem = pl.BlockSpec(memory_space=pltpu.SMEM)
+    hbm = pl.BlockSpec(memory_space=pl.ANY)
     return pl.pallas_call(
         functools.partial(migrate_kernel, group, class_count, ranks),
         out_shape=jax.ShapeDtypeStruct((depths, tile_rows, width), jnp.float32),
-        in_specs=[vmem, smem, vmem, vmem, vmem],
+        in_specs=[hbm, vmem, hbm, vmem, vmem, vmem, vmem],
         out_specs=vmem,
         scratch_shapes=[
             pltpu.VMEM((depths + 1,) + plane, jnp.float32),
@@ -401,12 +470,20 @@
             pltpu.VMEM(plane, jnp.float32),
             square,
             square,
-            pltpu.VMEM(spectra.shape, jnp.float32),
+            pltpu.VMEM((ranks, tile_rows, SUBS, width), jnp.float32),
             pltpu.VMEM((depths, ranks * 16, width), jnp.float32),
             pltpu.VMEM((depths, ranks - 1, 16, width), jnp.float32),
+            pltpu.VMEM((tile_rows, record_duration, width), jnp.bfloat16),
+            pltpu.VMEM((ranks, tile_rows, SUBS, width), jnp.float32),
+            pltpu.VMEM((2 * group, record_duration), jnp.float32),
+            pltpu.VMEM((2, SUBS, LANES), jnp.int32),
+            pltpu.VMEM((SUBS, LANES), jnp.float32),
+            pltpu.VMEM((group, degrees, SUBS, LANES), jnp.float32),
+            pltpu.VMEM((degrees, SUBS, LANES), jnp.float32),
             pltpu.SemaphoreType.DMA,
-            pltpu.SemaphoreType.DMA((ranks - 1,)),
-            pltpu.SemaphoreType.DMA((ranks - 1,)),
+            pltpu.SemaphoreType.DMA((tile_rows // 2,)),
+            pltpu.SemaphoreType.DMA((2, ranks - 1)),
+            pltpu.SemaphoreType.DMA((2, ranks - 1)),
             pltpu.SemaphoreType.DMA((depths, ranks - 1)),
             pltpu.SemaphoreType.DMA((depths, ranks - 1)),
         ],
@@ -414,7 +491,15 @@
             collective_id=0, has_side_effects=True, vmem_limit_bytes=VMEM_BYTES
         ),
         name="migrate",
-    )(off, wave, tab, classes, spectra)
+    )(
+        records[0].transpose(1, 0, 2),
+        narrow,
+        jnp.asarray(pair),
+        wavelet,
+        offsets[0].transpose(1, 2, 0),
+        coefficients.transpose(1, 3, 2, 0),
+        classes,
+    )
 
 
 def dft_table(count, record_duration):

time: 59.1 us -> 51.1 us (0.86)
  matrix products: 3.39 us -> 0 us
  local copies, waits for them, and re-layouts: 3.4 us -> 1.38 us
  other arithmetic: 1.6 us -> 0 us
  Pallas kernels: 50.4 us -> 49.5 us
    dot_general x2 -> x0, matrix products: 3.39 us -> none  [the longest x1 2.41 us: fast_device(): jnp.einsum('jqt,txy->jxqy', narrow, records[0], preferred_element_type=jn...]
    reduce_sum x1 -> x0, other arithmetic: 1.6 us -> none  [fast_device(): wave = jnp.sum(mine * wavelet, axis=1)]
    pallas_call x1, Pallas kernels: 50.4 us -> 49.5 us  [fast_device(): pl.pallas_call(functools.partial(migrate_kernel, group, class_count, rank...]
    reshape x2 -> x0, local copies, waits for them, and re-layouts: 0.72 us -> none  [fast_device(): tab = tab.reshape(2, degrees, group * class_count)]
    unnamed x3 -> x0, local copies, waits for them, and re-layouts: 0.7 us -> none
    pad x1 -> x0, local copies, waits for them, and re-layouts: 0.6 us -> none  [fast_device(): off = jnp.pad(off, ((0, 0), (0, 0), (0, LANES - off.shape[2])))]
where the time goes in v3:
time: 51.1 us; the launch traced here: 50.9 us
  Pallas kernels  49.5 us (97%)
  local copies, waits for them, and re-layouts  1.38 us (3%)
    pallas_call x1, Pallas kernels, fast_device(): pl.pallas_call(functools.partial(migrate_kernel, group, class_count, rank...  49.5 us
    pallas_call x1, local copies, waits for them, and re-layouts, fast_device(): pl.pallas_call(functools.partial(migrate_kernel, group, class_count, rank...  1.38 us

profile of v3, /device:TPU:0, one launch (start us, length us, event | category | flops | bytes accessed | tf_op | source)
XLA Modules:
  0.0 50.9 jit_solution(15768141771708930444)
XLA Ops:
  0.0 49.5 %migrate.1 = f32[4,12,128]{2,1,0:T(8,128)} custom-call(bf16[12,1024,128]{2,1,0:T(8,128)(2,1)} %bitcast.7, bf16[128,1024]{1,0:T(8,128)(2,1)} %constant.10.table, f32[16,8,1024]{2,1,0:T(8,128)} %constant.5.clone.moments_all, f32[1,1024]{1,0:T(1,128)} %wavelet.1, s32[8,2,12]{2,1,0:T(2,128)} %bitcast.9, f32[4,9,2,32]{3,2,1,0:T(2,128)} %bitcast.8, ...), custom_call_target="tpu_custom_call" | custom-call | tf_op jit(solution)/shard_map/migrate/pallas_call | solution.py:461
  49.5 1.4 %copy.8 = f32[4,12,128]{2,0,1:T(4,128)} copy(f32[4,12,128]{2,1,0:T(8,128)} %migrate.1) | data formatting | bytes 49152 | tf_op jit(solution)/shard_map/migrate/pallas_call | solution.py:461

commit v4 on v3

--- a/solution.py
+++ b/solution.py
@@ -82,7 +82,7 @@
     for n in range(0, len(places), group):
         some = places[n : n + group]
         rows = [classes[d, pl.ds(x, blocks, stride=nx), :] for d, x in some]
-        slot = n // group % 2
+        slot = n // group
         flat[slot] = jnp.transpose(jnp.concatenate(rows, axis=0).astype(jnp.float32))
         for i, (d, x) in enumerate(some):
             for y in range(ny):
@@ -90,15 +90,21 @@
                 idx[d, x, y] = pick(line, lane // group + i * blocks) + lane % group * class_count
 
 
-def look_up(tab, idx, filters, x, y):
-    degrees = tab.shape[0]
+def look_up(tab, idx, store, x, y):
     place = idx[x, y]
-    for k in range(degrees):
+    for k in range(tab.shape[0]):
         for part in range(2):
-            filters[k, part, x, y] = pick(row_of(tab, part, k), place)
-
-
-def degree_pass(old, cur, planes, acc, filters, node, group, nx, ny, begin=None, beside=None):
+            store(k, part, pick(row_of(tab, part, k), place))
+
+
+def planes_at(filters, x, y):
+    def store(k, part, value):
+        filters[k, part, x, y] = value
+
+    return store
+
+
+def degree_pass(old, cur, planes, acc, filters, node, group, nx, ny, begin=None, beside=None, kept=None):
     lane, sub = iotas()
     low, high = lane >= group, lane < LANES - group
     first, last = sub >= 1, sub < SUBS - 1
@@ -132,6 +138,9 @@
                 held = [old[c, x, y] for x in range(nx)]
                 total = [t - node * h for t, h in zip(total, held)]
                 was.append(held)
+                if kept is not None:
+                    for x in range(nx):
+                        kept[c, x, y] = held[x]
             for x in range(nx):
                 cur[c, x, y] = total[x]
             made.append(total)
@@ -165,25 +174,38 @@
 def spread_ahead(ahead, steps, j, nx, ny):
     if ahead is None:
         return None
-    share = nx * ny // steps
+    tab, idx, filters, staged = ahead
+    share, slots = nx * ny // steps, 0 if staged is None else staged.shape[0]
+
+    def at(n):
+        return n % nx, j * (share // nx) + n // nx
+
+    def flush(n):
+        for k in range(tab.shape[0]):
+            for part in range(2):
+                filters[(k, part) + at(n)] = staged[n % slots, k, part]
 
     def beside(y):
         for n in range(share * y // ny, share * (y + 1) // ny):
-            ahead(n % nx, j * (share // nx) + n // nx)
+            if staged is None:
+                look_up(tab, idx, planes_at(filters, *at(n)), *at(n))
+                continue
+            if n >= slots:
+                flush(n - slots)
+
+            def store(k, part, value):
+                staged[n % slots, k, part] = value
+
+            look_up(tab, idx, store, *at(n))
+        if y == ny - 1 and staged is not None:
+            for n in range(share - slots, share):
+                flush(n)
 
     return beside
 
 
-def all_degrees(cur, planes, acc, filters, group, nx, ny, ahead=None, begin=None):
+def all_degrees(cur, planes, acc, filters, group, nx, ny, ahead=None, fresh=False, kept=None):
     steps = filters.shape[0] - 1
-    done = 0
-    if begin is not None:
-        degree_pass(
-            begin, cur, planes, acc, filters.at[1], 16.0 * NODES[0], group, nx, ny,
-            filters.at[0], spread_ahead(ahead, steps, 0, nx, ny),
-        )
-        done = 1
-
     def one(shifted, j, carry):
         degree_pass(
             cur, cur, planes, acc, filters.at[j + 1], node_at(j) if shifted else None,
@@ -191,14 +213,19 @@
         )
         return carry
 
-    if len(NODES) - done == 1:
-        one(True, done, 0)
+    done = 0
+    if fresh:
+        degree_pass(
+            acc, cur, planes, acc, filters.at[1], 16.0 * NODES[0], group, nx, ny,
+            filters.at[0], spread_ahead(ahead, steps, 0, nx, ny), kept,
+        )
+        one(True, 1, 0)
     else:
-        lax.fori_loop(done, len(NODES), functools.partial(one, True), 0)
+        lax.fori_loop(0, len(NODES), functools.partial(one, True), 0)
     lax.fori_loop(len(NODES), steps, functools.partial(one, False), 0)
 
 
-def source_steps(group, off_ref, wave, tab, out, idx, filters, cur):
+def source_steps(group, off_ref, wave, tab, out, kept, idx, filters, cur, staged):
     depths, nx, ny = idx.shape[:3]
     lane, _ = iotas()
 
@@ -211,16 +238,16 @@
             hit = (row_x[x] % SPACING == off_x[x]) & (off_y[x] == y)
             v = jnp.where(hit, 1.0, 0.0)
             cur[0, x, y] = v
-            out[0, 0, x, y] = filters[0, 0, 0, x, y] * v
-            out[0, 1, x, y] = filters[0, 0, 1, x, y] * v
+            out[0, x, y] = filters[0, 0, 0, x, y] * v
+            out[1, x, y] = filters[0, 0, 1, x, y] * v
         return carry
 
     lax.fori_loop(0, ny, spike_row, 0, unroll=2)
 
-    def ahead_of(d):
-        return functools.partial(look_up, tab, idx.at[d], filters.at[d])
-
-    all_degrees(cur, 1, out.at[0], filters.at[0], group, nx, ny, ahead_of(1))
+    def ahead_of(d, staged=None):
+        return tab, idx.at[d], filters.at[d], staged
+
+    all_degrees(cur, 1, out, filters.at[0], group, nx, ny, ahead_of(1))
     wr, wi = jnp.zeros((SUBS, LANES), jnp.float32), jnp.zeros((SUBS, LANES), jnp.float32)
     for f in range(group):
         wr = jnp.where(lane % group == f, jnp.broadcast_to(wave[pl.ds(f, 1), :], wr.shape), wr)
@@ -230,23 +257,23 @@
 
     def wave_row(y, carry):
         for x in range(nx):
-            re, im = out[0, 0, x, y], out[0, 1, x, y]
-            out[0, 0, x, y] = wr * re - wi * im
-            out[0, 1, x, y] = wr * im + wi * re
+            re, im = out[0, x, y], out[1, x, y]
+            out[0, x, y] = wr * re - wi * im
+            out[1, x, y] = wr * im + wi * re
         return carry
 
     lax.fori_loop(0, ny, wave_row, 0, unroll=2)
 
     def depth(d, carry):
-        filter_step(group, cur, out.at[d - 1], out.at[d], filters.at[d], ahead_of(d + 1))
+        filter_step(group, cur, out, filters.at[d], kept.at[d - 1], ahead_of(d + 1))
         return carry
 
     lax.fori_loop(1, depths - 1, depth, 0)
 
 
-def filter_step(group, cur, begin, end, filters, ahead=None):
-    nx, ny = begin.shape[1:3]
-    all_degrees(cur, 2, end, filters, group, nx, ny, ahead, begin)
+def filter_step(group, cur, field, filters, kept, ahead=None):
+    nx, ny = field.shape[1:3]
+    all_degrees(cur, 2, field, filters, group, nx, ny, ahead, True, kept)
 
 
 def small_tables(offsets, wavelet, coefs, off, wave, tab, wide, moments):
@@ -315,20 +342,20 @@
     for x in range(nx):
         for y in range(ny):
             v = src[0, x, y] * acc[0, x, y] - src[1, x, y] * acc[1, x, y]
-            flat[x % 2, pl.ds(y, SUBS, stride=ny), :] = v
-        turned[x % 2] = jnp.transpose(flat[x % 2])
+            flat[x, pl.ds(y, SUBS, stride=ny), :] = v
+        turned[x] = jnp.transpose(flat[x])
         for b in range(2):
-            total = turned[x % 2, pl.ds(b * group, owners, stride=2 * group), :]
+            total = turned[x, pl.ds(b * group, owners, stride=2 * group), :]
             for f in range(1, group):
-                total = total + turned[x % 2, pl.ds(b * group + f, owners, stride=2 * group), :]
+                total = total + turned[x, pl.ds(b * group + f, owners, stride=2 * group), :]
             image[pl.ds(b * nx + x, owners, stride=16), :] = total
 
 
 def migrate_kernel(
     group, class_count, ranks,
     records, table, moments_all, wavelet, offsets, coefs, classes,
-    out,
-    fields, idx, filters, cur, flat, turned, received, image, slots,
+    near, rest,
+    fields, kept, idx, filters, staged, cur, flat, turned, received, image, slots,
     traces, spectra, moments, off, wave, wide, tab,
     local_sem, rec_sem, a_send, a_recv, i_send, i_recv,
 ):
@@ -382,7 +409,7 @@
             share = nx * ny // (halves * pairs)
             for n in range(share):
                 at = p * share + n
-                look_up(tab, idx.at[0], filters.at[0], at // ny, at % ny)
+                look_up(tab, idx.at[0], planes_at(filters.at[0], at // ny, at % ny), at // ny, at % ny)
             return carry
 
         lax.fori_loop(0, pairs, pair, 0)
@@ -393,13 +420,13 @@
     lax.fori_loop(0, halves, transform, 0)
     own = pltpu.make_async_copy(spectra.at[me], received.at[me], local_sem)
     own.start()
-    source_steps(group, off, wave, tab, fields, idx, filters, cur)
-    acc = fields.at[depths]
+    source_steps(group, off, wave, tab, fields.at[0], kept, idx, filters, cur, staged)
+    acc = fields.at[1]
 
     def sends(d):
         return [
             remote(
-                image.at[d, pl.ds(peer * 16, 16)],
+                image.at[d, pl.ds(peer * 16, tile)],
                 slots.at[d, k],
                 i_send.at[d, k],
                 i_recv.at[d, k],
@@ -415,17 +442,17 @@
             for half in range(halves):
                 for copy in spread(half):
                     copy.wait()
+            kept[depths - 1] = fields[0]
             unpack_received(received, acc, flat, group, nx, ny)
 
         ready = jnp.minimum(n, 1)
-        begin = (depths - 2) * (1 - ready) + depths * ready
-        end = depths - 1 + ready
         d = (depths - 1) * (1 - ready) + (n - 1) * ready
-        filter_step(group, cur, fields.at[begin], fields.at[end], filters.at[d])
+        spare = (depths - 2) * (1 - ready) + depths * ready
+        filter_step(group, cur, fields.at[ready], filters.at[d], kept.at[spare])
 
         @pl.when(n >= 1)
         def _():
-            form_image(fields.at[d], acc, flat, turned, image.at[d], group, nx, ny)
+            form_image(kept.at[d], acc, flat, turned, image.at[d], group, nx, ny)
             for copy in sends(d):
                 copy.start()
 
@@ -433,14 +460,16 @@
 
     lax.fori_loop(0, depths + 1, step, 0)
     for d in range(depths):
-        total = image[d, pl.ds(me * 16, 16), :]
-        for k, copy in enumerate(sends(d)):
+        copies = sends(d)
+        for copy in copies:
+            copy.wait_send()
+        sums = [image[d, pl.ds(me * 16, tile), :], None]
+        for k, copy in enumerate(copies):
             copy.wait_recv()
-            total = total + slots[d, k]
-        out[d] = total[:tile]
-    for d in range(depths):
-        for copy in sends(d):
-            copy.wait_send()
+            n = k * 2 // ranks
+            sums[n] = slots[d, k] if sums[n] is None else sums[n] + slots[d, k]
+        near[:, d, :] = sums[0]
+        rest[:, d, :] = sums[1]
 
 
 def fast_device(records, wavelet, offsets, classes, coefficients):
@@ -455,24 +484,26 @@
     ).reshape(ranks, 2 * group, record_duration)
     narrow = jnp.asarray(pair.reshape(2 * NF, record_duration)).astype(jnp.bfloat16)
     plane = (2, nx, ny, SUBS, LANES)
-    square = pltpu.VMEM((2, LANES, LANES), jnp.float32)
+    square = pltpu.VMEM((depths * nx // group, LANES, LANES), jnp.float32)
     vmem = pl.BlockSpec(memory_space=pltpu.VMEM)
     hbm = pl.BlockSpec(memory_space=pl.ANY)
-    return pl.pallas_call(
+    near, rest = pl.pallas_call(
         functools.partial(migrate_kernel, group, class_count, ranks),
-        out_shape=jax.ShapeDtypeStruct((depths, tile_rows, width), jnp.float32),
+        out_shape=[jax.ShapeDtypeStruct((tile_rows, depths, width), jnp.float32)] * 2,
         in_specs=[hbm, vmem, hbm, vmem, vmem, vmem, vmem],
-        out_specs=vmem,
+        out_specs=[vmem] * 2,
         scratch_shapes=[
+            pltpu.VMEM((2,) + plane, jnp.float32),
             pltpu.VMEM((depths + 1,) + plane, jnp.float32),
             pltpu.VMEM((depths,) + plane[1:], jnp.int32),
             pltpu.VMEM((depths, degrees) + plane, jnp.float32),
+            pltpu.VMEM((2, degrees, 2, SUBS, LANES), jnp.float32),
             pltpu.VMEM(plane, jnp.float32),
             square,
             square,
             pltpu.VMEM((ranks, tile_rows, SUBS, width), jnp.float32),
             pltpu.VMEM((depths, ranks * 16, width), jnp.float32),
-            pltpu.VMEM((depths, ranks - 1, 16, width), jnp.float32),
+            pltpu.VMEM((depths, ranks - 1, tile_rows, width), jnp.float32),
             pltpu.VMEM((tile_rows, record_duration, width), jnp.bfloat16),
             pltpu.VMEM((ranks, tile_rows, SUBS, width), jnp.float32),
             pltpu.VMEM((2 * group, record_duration), jnp.float32),
@@ -500,6 +531,7 @@
         coefficients.transpose(1, 3, 2, 0),
         classes,
     )
+    return (near + rest).transpose(1, 0, 2)
 
 
 def dft_table(count, record_duration):

time: 51.1 us -> 48.5 us (0.949)
  Pallas kernels: 49.5 us -> 46.9 us
  local copies, waits for them, and re-layouts: 1.38 us -> 0 us
  other arithmetic: 0 us -> 1.37 us
    pallas_call x1, Pallas kernels: 49.5 us -> 46.9 us  [fast_device(): pl.pallas_call(functools.partial(migrate_kernel, group, class_count, rank...]
    pallas_call x1 -> x0, local copies, waits for them, and re-layouts: 1.38 us -> none  [fast_device(): pl.pallas_call(functools.partial(migrate_kernel, group, class_count, rank...]
    transpose x0 -> x1, other arithmetic: none -> 1.37 us  [fast_device(): return (near + rest).transpose(1, 0, 2)]
where the time goes in v4:
time: 48.5 us; the launch traced here: 48.3 us
  Pallas kernels  46.9 us (97%)
  other arithmetic  1.37 us (3%)
    pallas_call x1, Pallas kernels, fast_device(): pl.pallas_call(functools.partial(migrate_kernel, group, class_count, rank...  46.9 us
    transpose x1, other arithmetic, fast_device(): return (near + rest).transpose(1, 0, 2)  1.37 us

profile of v4, /device:TPU:0, one launch (start us, length us, event | category | flops | bytes accessed | tf_op | source)
XLA Modules:
  0.0 48.3 jit_solution(2908303647564858773)
XLA Ops:
  0.0 46.9 %migrate.1 = (f32[12,4,128]{2,1,0:T(4,128)}, f32[12,4,128]{2,1,0:T(4,128)}) custom-call(bf16[12,1024,128]{2,1,0:T(8,128)(2,1)} %bitcast.9, bf16[128,1024]{1,0:T(8,128)(2,1)} %constant.10.table, f32[16,8,1024]{2,1,0:T(8,128)} %constant.5.clone.moments_all, f32[1,1024]{1,0:T(1,128)} %wavelet.1, s32[8,2,12]{2,1,0:T(2,128)} %bitcast.11, ...), custom_call_target="tpu_custom_call" | custom-call | tf_op jit(solution)/shard_map/migrate/pallas_call | solution.py:490
  46.9 1.4 %add_bitcast_fusion = f32[4,12,128]{2,0,1:T(4,128)} fusion(f32[12,4,128]{2,1,0:T(4,128)} %get-tuple-element.7, f32[12,4,128]{2,1,0:T(4,128)} %get-tuple-element.8), kind=kLoop, calls=%fused_computation | loop fusion | flops 6144 | bytes 73728 | tf_op jit(solution)/shard_map/transpose | solution.py:534

commit v5 on v4

--- a/solution.py
+++ b/solution.py
@@ -242,12 +242,12 @@
             out[1, x, y] = filters[0, 0, 1, x, y] * v
         return carry
 
-    lax.fori_loop(0, ny, spike_row, 0, unroll=2)
+    lax.fori_loop(0, ny, spike_row, 0, unroll=4)
 
     def ahead_of(d, staged=None):
         return tab, idx.at[d], filters.at[d], staged
 
-    all_degrees(cur, 1, out, filters.at[0], group, nx, ny, ahead_of(1))
+    all_degrees(cur, 1, out, filters.at[0], group, nx, ny, ahead_of(1, staged))
     wr, wi = jnp.zeros((SUBS, LANES), jnp.float32), jnp.zeros((SUBS, LANES), jnp.float32)
     for f in range(group):
         wr = jnp.where(lane % group == f, jnp.broadcast_to(wave[pl.ds(f, 1), :], wr.shape), wr)
@@ -262,7 +262,7 @@
             out[1, x, y] = wr * im + wi * re
         return carry
 
-    lax.fori_loop(0, ny, wave_row, 0, unroll=2)
+    lax.fori_loop(0, ny, wave_row, 0, unroll=4)
 
     def depth(d, carry):
         filter_step(group, cur, out, filters.at[d], kept.at[d - 1], ahead_of(d + 1))

time: 48.5 us -> 47.5 us (0.979)
  Pallas kernels: 46.9 us -> 45.9 us
    pallas_call x1, Pallas kernels: 46.9 us -> 45.9 us  [fast_device(): pl.pallas_call(functools.partial(migrate_kernel, group, class_count, rank...]
where the time goes in v5:
time: 47.5 us; the launch traced here: 47.3 us
  Pallas kernels  45.9 us (97%)
  other arithmetic  1.37 us (3%)
    pallas_call x1, Pallas kernels, fast_device(): pl.pallas_call(functools.partial(migrate_kernel, group, class_count, rank...  45.9 us
    transpose x1, other arithmetic, fast_device(): return (near + rest).transpose(1, 0, 2)  1.37 us

profile of v5, /device:TPU:0, one launch (start us, length us, event | category | flops | bytes accessed | tf_op | source)
XLA Modules:
  0.0 47.3 jit_solution(12201545817813820233)
XLA Ops:
  0.0 45.9 %migrate.1 = (f32[12,4,128]{2,1,0:T(4,128)}, f32[12,4,128]{2,1,0:T(4,128)}) custom-call(bf16[12,1024,128]{2,1,0:T(8,128)(2,1)} %bitcast.9, bf16[128,1024]{1,0:T(8,128)(2,1)} %constant.10.table, f32[16,8,1024]{2,1,0:T(8,128)} %constant.5.clone.moments_all, f32[1,1024]{1,0:T(1,128)} %wavelet.1, s32[8,2,12]{2,1,0:T(2,128)} %bitcast.11, ...), custom_call_target="tpu_custom_call" | custom-call | tf_op jit(solution)/shard_map/migrate/pallas_call | solution.py:490
  45.9 1.4 %add_bitcast_fusion = f32[4,12,128]{2,0,1:T(4,128)} fusion(f32[12,4,128]{2,1,0:T(4,128)} %get-tuple-element.7, f32[12,4,128]{2,1,0:T(4,128)} %get-tuple-element.8), kind=kLoop, calls=%fused_computation | loop fusion | flops 6144 | bytes 73728 | tf_op jit(solution)/shard_map/transpose | solution.py:534
